TPU v7x, 512 devices: a whole 4x4x16 slice. The times are simulated.
512 devices in a mesh: pa: 128 (over x_lo, z, y), sa: 4 (over x_hi, core).
Axes of the slice: x: 4 (x_hi: 2, x_lo: 2; x = x_hi * 2 + x_lo), y: 4, z: 16, core: 2. Of those that a mesh axis runs over, the one named last changes fastest.
Arguments:
- raw_echo: bfloat16 [4096, 2, 32768], P('pa', None, 'sa'), may hold values from -6 to 6
- chirp_replica: bfloat16 [2, 1024], replicated, may hold values from -0.125 to 0.125
- azimuth_refs: bfloat16 [1024, 2, 512], P('pa'), may hold values from -0.1875 to 0.1875
- migration_index: int32 [4, 128], replicated, may hold values from 0 to 1023
- window_start: int32 [1], replicated, may hold values from 0 to 2047
Outputs:
- image: float32 [4, 4096, 2, 4096], P('sa', 'pa')
All inputs are finite; a program needn't handle non-finite values.
Results may differ from a plain program's by a relative error of at most 0.0029.
Values may be sent and summed in bfloat16 or wider, within the bound.
A program may use at most 64 MiB of HBM per device.

v0:
```python
import jax
import jax.numpy as jnp
from jax import lax
from jax.sharding import PartitionSpec as P

R = 16384
L = 512
RB = 256


def passed_along(value, axis, steps):
    count = lax.axis_size(axis)
    initial, last = (max(0, -steps), min(count, count - steps))
    return lax.ppermute(value, axis, [(source, source + steps) for source in range(initial, last)])


def toeplitz(diagonal_taps, size):
    span_size = 2 * size - 1
    reversed_taps = diagonal_taps[..., ::-1]
    shifted = jnp.concatenate(
        [reversed_taps[..., size - 1 :], reversed_taps[..., : size - 1]], axis=-1
    )
    reps = (1,) * (shifted.ndim - 1) + (size,)
    tiled_flat = jnp.tile(shifted, reps)[..., : size * (span_size - 1)]
    return tiled_flat.reshape(shifted.shape[:-1] + (size, span_size - 1))[..., :size]


def tap_blocks(tap_values, size):
    block_total = tap_values.shape[1] // size + 1
    padded_taps = jnp.pad(tap_values, ((0, 0), (size, 2 * size)))
    matrices = []
    for offset_block in range(block_total):
        first_tap = offset_block * size + 1
        parts = toeplitz(padded_taps[:, first_tap : first_tap + 2 * size - 1], size)
        real_part = parts[0]
        imag_part = parts[1]
        matrices.append(
            jnp.stack([jnp.stack([real_part, -imag_part]), jnp.stack([imag_part, real_part])])
        )
    return jnp.stack(matrices)


def correlate(blocked, matrices, output_count):
    summed = jnp.zeros((blocked.shape[0], 2, output_count, blocked.shape[3]), jnp.float32)
    for offset_block in range(matrices.shape[0]):
        piece_rows = blocked[:, :, offset_block : offset_block + output_count, :]
        summed = summed + jnp.einsum(
            "rcib,cdbn->rdin",
            piece_rows,
            matrices[offset_block],
            preferred_element_type=jnp.float32,
        )
    return summed


def compress(samples, matrices, output_count):
    pulse_count = samples.shape[0]
    blocked = samples.reshape(pulse_count, 2, -1, RB)
    focused = correlate(blocked, matrices, output_count)
    return focused.astype(jnp.bfloat16).reshape(pulse_count, 2, output_count * RB)


def cut_slots(source_data, base_offset, stride, length, slot_count):
    padded = jnp.pad(source_data, ((0, 0), (0, 0), (length, length)))
    limit = source_data.shape[2] + length
    slot_list = []
    for target in range(slot_count):
        slot_offset = jnp.clip(base_offset + target * stride + length, 0, limit)
        slot_list.append(lax.dynamic_slice_in_dim(padded, slot_offset, length, 2))
    return jnp.stack(slot_list)


def on_device(raw_echo, chirp_replica, azimuth_refs, migration_index, window_start):
    segment = raw_echo.shape[2]
    segment_devices = lax.axis_size("sa")
    pulse_devices = lax.axis_size("pa")
    sub_index = lax.axis_index("sa")
    bin_owner = lax.axis_index("pa")
    tap_count = chirp_replica.shape[1]
    kept_width = R // segment_devices
    window_first = window_start[0]
    range_mats = tap_blocks(chirp_replica, RB)
    base_offset = window_first - sub_index * segment
    next_edge = passed_along(raw_echo[:, :, :tap_count], "sa", -1)
    extended = jnp.concatenate([raw_echo, next_edge], axis=2)
    compressed = compress(extended, range_mats, segment // RB)
    slot_stack = cut_slots(compressed, base_offset, kept_width, kept_width, segment_devices)
    incoming = lax.all_to_all(slot_stack, "sa", split_axis=0, concat_axis=0, tiled=True)
    kept_bins = jnp.sum(incoming.astype(jnp.float32), axis=0).astype(jnp.bfloat16)
    pulse_count = kept_bins.shape[0]
    bin_count = kept_width // pulse_devices
    outgoing = jnp.transpose(kept_bins, (2, 1, 0)).reshape(pulse_devices, bin_count, 2, pulse_count)
    turned = lax.all_to_all(outgoing, "pa", split_axis=0, concat_axis=3, tiled=True)
    range_lines = turned[0]
    row_index = migration_index[sub_index, bin_owner]
    shard_piece = lax.all_gather(azimuth_refs, "pa", axis=0, tiled=True)
    row_ids = jnp.arange(shard_piece.shape[0])
    selector = (row_ids == row_index).astype(jnp.float32)
    chosen = jnp.tensordot(selector, shard_piece.astype(jnp.float32), axes=1)
    reference_row = chosen.astype(jnp.bfloat16)
    block_size = L // 2
    az_mats = tap_blocks(reference_row, block_size)
    total_pulses = range_lines.shape[2]
    block_count = total_pulses // block_size
    blocked = range_lines.reshape(bin_count, 2, block_count, block_size)
    blocked = jnp.pad(blocked, ((0, 0), (0, 0), (1, 1), (0, 0)))
    focused = correlate(blocked, az_mats, block_count)
    return focused.reshape(1, bin_count, 2, total_pulses)


def solution(mesh):
    placed = (P("pa", None, "sa"), P(), P("pa", None, None), P(), P())
    return jax.shard_map(
        on_device, mesh=mesh, in_specs=placed, out_specs=P("sa", "pa", None, None), check_vma=False
    )
```

profile of v0, /device:TPU:4, one launch (start us, length us, event | category | flops | bytes accessed | tf_op | source)
XLA Modules:
  0.0 632.4 jit_solution(3211251255467756287)
XLA Ops:
  6.5 1.6 slice.253
  8.2 1.9 collective-permute-start
  12.3 1.5 tile.35
  14.2 1.0 reshape.70
  15.8 1.5 tile.37
  17.7 1.0 reshape.72
  19.3 1.5 tile.39
  21.2 1.0 reshape.73
  22.8 1.5 tile.81
  24.7 1.0 reshape.74
  26.4 1.5 tile.83
  28.3 1.0 reshape.75
  32.7 2.0 pad_maximum_fusion.1
  41.9 31.6 %all_to_all.20 = bf16[4,32,2,4096]{3,1,2,0:T(8,128)(2,1)S(1)} all-to-all(bf16[4,32,2,4096]{3,1,2,0:T(8,128)(2,1)S(1)} %pad_maximum_fusion), channel_id=1, replica_groups=mesh['pa'=128,'sa'=4] {'sa'}, dimensions={0} | all-to-all | bytes 4194304 | tf_op jit(solution)/shard_map/all_to_all | solution.py:88
  73.9 1.6 reshape.77
  75.5 2.7 copy.83
  78.2 4.4 reshape.109
  82.6 18.6 %all-to-all-start.1 = ((bf16[128,2,1024]{2,1,0:T(2,128)(2,1)}), bf16[128,2,1024]{2,1,0:T(2,128)(2,1)S(1)}, u32[]{:S(2)}, u32[]{:S(2)}) async-start(bf16[128,2,1024]{2,1,0:T(2,128)(2,1)} %reshape.109), calls=%async_computation.1 | async-start | bytes 1048576 | tf_op jit(solution)/shard_map/all_to_all | solution.py:93
  101.2 1.3 dynamic_slice.15
  103.2 34.5 %all-to-all-done.1 = bf16[128,2,1024]{2,1,0:T(2,128)(2,1)S(1)} async-done(((bf16[128,2,1024]{2,1,0:T(2,128)(2,1)}), bf16[128,2,1024]{2,1,0:T(2,128)(2,1)S(1)}, u32[]{:S(2)}, u32[]{:S(2)}) %all-to-all-start.1) | async-done | bytes 524320 | tf_op jit(solution)/shard_map/all_to_all | solution.py:93
  138.6 1.7 bitcast_bitcast_fusion
  140.4 4.9 copy.46
  145.3 1.5 reshape_squeeze.3
  147.0 462.0 %all-gather.2.cloned.1.call-done = bf16[1024,2,512]{2,1,0:T(2,128)(2,1)} async-done(((bf16[8,2,512]{2,1,0:T(2,128)(2,1)}), bf16[1024,2,512]{2,1,0:T(2,128)(2,1)}) %all-gather.2.cloned.1.call-update) | async-done | bytes 2097168 | tf_op jit(solution)/shard_map/all_gather | solution.py:96
  609.0 2.0 fusion.1
  611.7 1.5 tile.33
  613.6 1.0 reshape.69
  615.2 1.5 tile.85
  617.1 1.0 reshape.78
  618.6 1.5 tile.87
  620.5 1.0 reshape.79
  623.7 1.7 reshape.108
  (100 shorter events, 23.1 us)
Async XLA Ops:
  6.5 602.5 %all-gather.2.cloned.1.call-start = ((), (), s32[]{:S(2)}) async-start(), calls=%async_computation.2 | async-start | bytes 2113536 | tf_op jit(solution)/shard_map/all_gather | solution.py:96
  8.2 24.5 %collective-permute-start = (bf16[32,2,1024]{2,1,0:T(2,128)(2,1)}, bf16[32,2,1024]{2,1,0:T(2,128)(2,1)}, u32[]{:S(2)}, u32[]{:S(2)}) collective-permute-start(bf16[32,2,1024]{2,1,0:T(2,128)(2,1)} %slice.253), channel_id=1, source_target_pairs={{1,0},{2,1},{3,2},{5,4},{6,5},{7,6},{9,8},{10,9},{11,10},{13,12},{... | collective-permute-start | bytes 393224 | tf_op jit(solution)/shard_map/ppermute | solution.py:14
  29.4 3.3 copy-start
  35.5 1.0 copy-start.1
  35.5 1.0 copy-start.2
  36.5 0.9 copy-start.3
  36.5 1.0 copy-start.4
  37.5 0.9 copy-start.5
  37.5 1.0 copy-start.6
  82.6 55.0 %all-to-all-start.1 = ((bf16[128,2,1024]{2,1,0:T(2,128)(2,1)}), bf16[128,2,1024]{2,1,0:T(2,128)(2,1)S(1)}, u32[]{:S(2)}, u32[]{:S(2)}) async-start(bf16[128,2,1024]{2,1,0:T(2,128)(2,1)} %reshape.109), calls=%async_computation.1 | async-start | bytes 1048576 | tf_op jit(solution)/shard_map/all_to_all | solution.py:93
Sparse Core Ops, SparseCore 0:
  10.2 598.7 all-gather.1
where the time goes:
time: 641 us; the launch traced here: 632 us
  waiting for transfers between devices  496 us (77%)
  local copies, waits for them, and re-layouts  55.8 us (9%)
  blocking collectives  31.6 us (5%)
  starting transfers between devices  20.5 us (3%)
  between operations  14.9 us (2%)
  matrix products  7.02 us (1%)
    all_gather x1, waiting for transfers between devices, on_device(): shard_piece = lax.all_gather(azimuth_refs, 'pa', axis=0, tiled=True)  462 us
    all_to_all x1, waiting for transfers between devices, on_device(): lax.all_to_all(outgoing, 'pa', split_axis=0, concat_axis=3, tiled=True)  34.5 us
    all_to_all x1, blocking collectives, on_device(): lax.all_to_all(slot_stack, 'sa', split_axis=0, concat_axis=0, tiled=True)  31.6 us
    all_to_all x1, starting transfers between devices, on_device(): lax.all_to_all(outgoing, 'pa', split_axis=0, concat_axis=3, tiled=True)  18.6 us
  transfers between devices with their start and end apart: 3, of which 2 were waited for; matrix products, arithmetic and copies ran while one was open for 8% of the time, Pallas kernels for 0%

commit v1 on v0

v1 whole, which is shorter than its diff:
```python
import functools

import jax
import jax.numpy as jnp
from jax import lax
from jax.experimental import pallas as pl
from jax.experimental.pallas import tpu as pltpu
from jax.sharding import PartitionSpec as P

MESH = pl.DeviceIdType.MESH
BF16 = jnp.bfloat16
F32 = jnp.float32
NT = (((1,), (1,)), ((), ()))
SPAN = 1664
HALO = 3072
VMEM = pl.BlockSpec(memory_space=pltpu.VMEM)
SMEM = pl.BlockSpec(memory_space=pltpu.SMEM)
ANY = pl.BlockSpec(memory_space=pl.ANY)


def taps_kernel(shift_ref, chirp_ref, out_ref):
    out_ref[...] = jnp.zeros_like(out_ref)
    shift = shift_ref[0]
    for part in range(2):
        row = jnp.concatenate([chirp_ref[part : part + 1, :], jnp.zeros((1, 256), F32)], axis=1)
        row = pltpu.roll(jnp.broadcast_to(row, (8, 1280)), shift, 1)[:1]
        base = pltpu.roll(jnp.broadcast_to(row, (128, 1280)), 0, 1, stride=1, stride_axis=0)
        base = base.astype(BF16)
        for y in range(4):
            for g in range(4):
                r0 = part * 128 + g * 32
                out_ref[y, r0 : r0 + 32, 128 * g : 128 * g + 1280] = base[32 * y : 32 * y + 32, :]


def range_kernel(base_ref, w_ref, taps_ref, out_ref):
    base = base_ref[0]

    def item(t, carry):
        pieces = []
        for c in range(2):
            for x in range(2):
                off = pl.multiple_of(base + (t // 4) * 4096 + x * 2048 + (t % 4) * 512, 128)
                pieces.append(w_ref[c, :, pl.ds(off, SPAN)])
        lhs = jnp.concatenate(pieces, axis=0)
        for y in range(4):
            got = lax.dot_general(lhs, taps_ref[y], NT, preferred_element_type=F32)
            real = (got[:64, :128] + got[64:, 128:]).astype(BF16)
            imag = (got[64:, :128] - got[:64, 128:]).astype(BF16)
            for x in range(2):
                out_ref[t, x, y, 0] = real[32 * x : 32 * x + 32]
                out_ref[t, x, y, 1] = imag[32 * x : 32 * x + 32]
        return carry

    lax.fori_loop(0, 8, item, 0)


def turn_kernel(y_ref, rows_ref, turned_ref, row_ref, xr, zs, rr, rs, rz, sx, rx, sz, rz_sem, srow, rrow, szrow, rzrow):
    pa = lax.axis_index("pa")
    sa = lax.axis_index("sa")
    xlo, z, y = pa // 64, (pa // 4) % 16, pa % 4
    xhi, core = sa // 2, sa % 2
    me_plane = xlo * 4 + y

    def plane(index):
        return ((index // 4) * 16 + z) * 4 + index % 4

    def line(index):
        return (xlo * 16 + index) * 4 + y

    barrier = pltpu.get_barrier_semaphore()

    def greet_plane(i, carry):
        dev = plane(i)

        @pl.when(jnp.logical_or(dev != pa, xhi != sa))
        def _():
            pl.semaphore_signal(barrier, inc=1, device_id=(dev, xhi), device_id_type=MESH)

        return carry

    lax.fori_loop(0, 8, greet_plane, 0)

    def greet_line(i, carry):
        dev = line((z + i) % 16)
        pl.semaphore_signal(barrier, inc=1, device_id=(dev, sa), device_id_type=MESH)
        return carry

    lax.fori_loop(1, 16, greet_line, 0)

    @pl.when(sa == 0)
    def _():
        pl.semaphore_wait(barrier, 30)

    @pl.when(sa == 1)
    def _():
        pl.semaphore_wait(barrier, 31)

    @pl.when(sa >= 2)
    def _():
        pl.semaphore_wait(barrier, 15)

    @pl.when(xhi == 0)
    def _():
        def row_send(i, carry):
            jj, d = i // 8, (i + me_plane) % 8
            there = jnp.logical_or(plane(d) != pa, 2 * core + jj != sa)

            @pl.when(there)
            def _():
                pltpu.make_async_remote_copy(
                    rows_ref.at[jj, d], rr.at[me_plane], srow, rrow,
                    device_id=(plane(d), 2 * core + jj), device_id_type=MESH,
                ).start()

            @pl.when(jnp.logical_not(there))
            def _():
                pltpu.make_async_copy(rows_ref.at[jj, d], rr.at[me_plane], rrow).start()

            return carry

        lax.fori_loop(0, 16, row_send, 0)

        def send(i, carry):
            t, d = i // 8, (i + me_plane) % 8
            jj, k = t // 4, t % 4
            there = jnp.logical_or(plane(d) != pa, 2 * core + jj != sa)

            @pl.when(there)
            def _():
                pltpu.make_async_remote_copy(
                    y_ref.at[t, d], xr.at[k, :, me_plane], sx, rx.at[k],
                    device_id=(plane(d), 2 * core + jj), device_id_type=MESH,
                ).start()

            @pl.when(jnp.logical_not(there))
            def _():
                pltpu.make_async_copy(y_ref.at[t, d], xr.at[k, :, me_plane], rx.at[k]).start()

            return carry

        lax.fori_loop(0, 64, send, 0)

    eye = (
        lax.broadcasted_iota(jnp.int32, (128, 128), 0) == lax.broadcasted_iota(jnp.int32, (128, 128), 1)
    ).astype(BF16)

    pltpu.make_async_copy(rr, rr, rrow).wait()
    total = rr[0].astype(F32)
    for source in range(1, 8):
        total = total + rr[source].astype(F32)
    rs[...] = total.astype(BF16)

    def row_pass(i, carry):
        dest = (z + i) % 16
        pltpu.make_async_remote_copy(
            rs.at[dest], rz.at[z], szrow, rzrow, device_id=(line(dest), sa), device_id_type=MESH
        ).start()
        return carry

    lax.fori_loop(1, 16, row_pass, 0)
    pltpu.make_async_copy(rs.at[z], rz.at[z], rzrow).start()

    def group(k, carry):
        pltpu.make_async_copy(xr.at[k], xr.at[k], rx.at[k]).wait()
        for c in range(2):
            pulses = xr[k, c].reshape(256, 128)
            flipped = lax.dot_general(eye, pulses, NT, preferred_element_type=F32).astype(BF16)
            for g in range(4):
                for x in range(2):
                    zs[4 * k + g, c, x] = flipped[32 * g : 32 * g + 32, 128 * x : 128 * x + 128]

        def pass_on(g, inner):
            dest = 4 * k + g

            @pl.when(dest != z)
            def _():
                pltpu.make_async_remote_copy(
                    zs.at[dest], turned_ref.at[:, :, z], sz, rz_sem,
                    device_id=(line(dest), sa), device_id_type=MESH,
                ).start()

            @pl.when(dest == z)
            def _():
                pltpu.make_async_copy(zs.at[dest], turned_ref.at[:, :, z], rz_sem).start()

            return inner

        lax.fori_loop(0, 4, pass_on, 0)
        return carry

    lax.fori_loop(0, 4, group, 0)

    pltpu.make_async_copy(rz, rz, rzrow).wait()
    total = rz[0].astype(F32)
    for source in range(1, 16):
        total = total + rz[source].astype(F32)
    row_ref[...] = total.astype(BF16)

    pltpu.make_async_copy(turned_ref, turned_ref, rz_sem).wait()
    pltpu.make_async_copy(zs.at[pl.ds(0, 15)], zs.at[pl.ds(0, 15)], sz).wait()
    pltpu.make_async_copy(rs.at[pl.ds(0, 15)], rs.at[pl.ds(0, 15)], szrow).wait()

    @pl.when(xhi == 0)
    def _():
        @pl.when(core == 0)
        def _():
            for i in range(8):
                src = y_ref.at[i, pl.ds(0, 7)] if i < 4 else y_ref.at[i]
                pltpu.make_async_copy(src, src, sx).wait()
            src = rows_ref.at[0, pl.ds(0, 7)]
            pltpu.make_async_copy(src, src, srow).wait()
            src = rows_ref.at[1]
            pltpu.make_async_copy(src, src, srow).wait()

        @pl.when(core == 1)
        def _():
            pltpu.make_async_copy(y_ref, y_ref, sx).wait()
            pltpu.make_async_copy(rows_ref, rows_ref, srow).wait()


def azimuth_kernel(turned_ref, row_ref, out_ref, lhs, taps):
    zeros = jnp.zeros((32, 256), BF16)
    for c in range(2):
        lhs[c, 0] = zeros
        lhs[c, 17] = zeros
        for block in range(16):
            for half in range(2):
                tile = turned_ref[c, block // 8, 2 * (block % 8) + half]
                lhs[c, block + 1, :, 128 * half : 128 * half + 128] = tile
    for part in range(2):
        row = jnp.concatenate([row_ref[part : part + 1, :].astype(F32), jnp.zeros((1, 512), F32)], axis=1)
        wide = pltpu.roll(jnp.broadcast_to(row, (256, 1024)), 0, 1, stride=1, stride_axis=0)
        taps[256 * part : 256 * part + 256, :] = wide[:, :768].astype(BF16)
    got = []
    for c in range(2):
        total = None
        for o in range(3):
            rows = lhs[c, o : o + 16].reshape(512, 256)
            piece = lax.dot_general(rows, taps[:, 256 * o : 256 * o + 256], NT, preferred_element_type=F32)
            total = piece if total is None else total + piece
        got.append(total)
    real = got[0][:, :256] + got[1][:, 256:]
    imag = got[1][:, :256] - got[0][:, 256:]
    for block in range(16):
        out_ref[0, :, 256 * block : 256 * block + 256] = real[32 * block : 32 * block + 32]
        out_ref[1, :, 256 * block : 256 * block + 256] = imag[32 * block : 32 * block + 32]


def params(**more):
    return pltpu.CompilerParams(vmem_limit_bytes=48 << 20, **more)


def on_device(raw_echo, chirp_replica, azimuth_refs, migration_index, window_start):
    pa = lax.axis_index("pa")
    sa = lax.axis_index("sa")
    start = window_start[0]
    base = (start // 128) * 128
    taps = pl.pallas_call(
        taps_kernel,
        out_shape=jax.ShapeDtypeStruct((4, 256, SPAN), BF16),
        in_specs=[SMEM, VMEM],
        out_specs=VMEM,
        compiler_params=params(),
        name="range_taps",
    )((start - base).reshape(1), chirp_replica.astype(F32))

    planar = jnp.transpose(raw_echo, (1, 0, 2))
    halo = lax.ppermute(planar[:, :, :HALO], "sa", [(1, 0), (2, 1)])
    window = jnp.concatenate([planar, halo], axis=2)
    packed = pl.pallas_call(
        range_kernel,
        out_shape=jax.ShapeDtypeStruct((8, 2, 4, 2, 32, 128), BF16),
        in_specs=[SMEM, VMEM, VMEM],
        out_specs=VMEM,
        compiler_params=params(),
        name="range_correlate",
    )(base.reshape(1), window, taps)

    wanted = lax.dynamic_slice_in_dim(migration_index, 2 * (sa % 2), 2, 0)
    wanted = wanted.reshape(2, 2, 16, 4).transpose(0, 1, 3, 2).reshape(256)
    chosen = (wanted[:, None] == 8 * pa + jnp.arange(8)[None, :]).astype(BF16)
    rows = jnp.dot(chosen, azimuth_refs.reshape(8, 1024), preferred_element_type=F32).astype(BF16)
    rows = rows.reshape(2, 8, 16, 8, 128)

    dma = pltpu.SemaphoreType.DMA
    turned, row = pl.pallas_call(
        turn_kernel,
        out_shape=(
            jax.ShapeDtypeStruct((2, 2, 16, 32, 128), BF16),
            jax.ShapeDtypeStruct((8, 128), BF16),
        ),
        in_specs=[VMEM, VMEM],
        out_specs=(ANY, VMEM),
        scratch_shapes=[
            pltpu.VMEM((4, 2, 8, 32, 128), BF16),
            pltpu.VMEM((16, 2, 2, 32, 128), BF16),
            pltpu.VMEM((8, 16, 8, 128), BF16),
            pltpu.VMEM((16, 8, 128), BF16),
            pltpu.VMEM((16, 8, 128), BF16),
            dma, dma((4,)), dma, dma, dma, dma, dma, dma,
        ],
        compiler_params=params(collective_id=0, has_side_effects=True),
        name="corner_turn",
    )(packed.reshape(8, 8, 2, 32, 128), rows)

    image = pl.pallas_call(
        azimuth_kernel,
        out_shape=jax.ShapeDtypeStruct((2, 32, 4096), F32),
        in_specs=[VMEM, VMEM],
        out_specs=VMEM,
        scratch_shapes=[pltpu.VMEM((2, 18, 32, 256), BF16), pltpu.VMEM((512, 768), BF16)],
        compiler_params=params(),
        name="azimuth_correlate",
    )(turned, row.reshape(2, 512))
    return jnp.transpose(image, (1, 0, 2))[None]


def solution(mesh):
    placed = (P("pa", None, "sa"), P(), P("pa", None, None), P(), P())
    return jax.shard_map(
        on_device, mesh=mesh, in_specs=placed, out_specs=P("sa", "pa", None, None), check_vma=False
    )
```

time: 641 us -> 80.9 us (0.13)
  the two profiles are of different devices: /device:TPU:4 before, /device:TPU:5 now
where the time goes in v1:
time: 80.9 us; the launch traced here: 80.8 us
  Pallas kernels  74.7 us (92%)
  local copies, waits for them, and re-layouts  4.06 us (5%)
  between operations  0.86 us (1%)
    pallas_call x1, Pallas kernels, on_device(): pl.pallas_call(turn_kernel, out_shape=(jax.ShapeDtypeStruct((2, 2, 16, 32...  63.3 us
    pallas_call x1, Pallas kernels, on_device(): pl.pallas_call(range_kernel, out_shape=jax.ShapeDtypeStruct((8, 2, 4, 2,...  9.8 us
    unnamed x9, local copies, waits for them, and re-layouts  1.95 us
    broadcast_in_dim x1, local copies, waits for them, and re-layouts, on_device(): return jnp.transpose(image, (1, 0, 2))[None]  1.78 us
  transfers between devices with their start and end apart: 1, of which 0 were waited for; matrix products, arithmetic and copies ran while one was open for 1% of the time, Pallas kernels for 1%

profile of v1, /device:TPU:5, one launch (start us, length us, event | category | flops | bytes accessed | tf_op | source)
XLA Modules:
  0.0 80.8 jit_solution(7646293302660812153)
XLA Ops:
  0.0 0.0 copy-start
  0.0 0.0 copy-start.2
  0.0 0.0 copy-start.1
  0.0 1.8 %copy.14 = bf16[32,2,8192]{2,0,1:T(8,128)(2,1)S(1)} copy(bf16[32,2,8192]{2,1,0:T(2,128)(2,1)} %param.5) | data formatting | bytes 2097152 | tf_op args[0]
  1.9 0.7 collective-permute-start
  3.3 0.0 copy-done.2
  3.3 0.0 copy-done.1
  3.3 0.0 copy-done
  3.4 0.1 reshape.30
  3.5 0.1 copy.9
  3.6 0.1 eq.17
  3.7 0.3 fusion
  4.0 0.1 copy.12
  4.1 0.5 range_taps.1.taps_ref
  4.6 0.0 collective-permute-done
  4.6 0.1 pad_maximum_fusion.w_ref
  4.7 9.8 %range_correlate.1 = bf16[8,2,4,2,32,128]{5,4,3,2,1,0:T(8,128)(2,1)S(1)} custom-call(s32[1]{0:T(128)} %bitcast.1.base_ref, bf16[2,32,11264]{2,1,0:T(8,128)(2,1)S(1)} %pad_maximum_fusion.w_ref, bf16[4,256,1664]{2,1,0:T(8,128)(2,1)S(1)} %range_taps.1.taps_ref), custom_call_target="tpu_custom_call" | custom-call | tf_op jit(solution)/shard_map/range_correlate/pallas_call | solution.py:270
  14.5 63.3 %corner_turn.1 = (bf16[2,2,16,32,128]{4,3,2,1,0:T(8,128)(2,1)S(1)}, bf16[8,128]{1,0:T(8,128)(2,1)S(1)}) custom-call(bf16[8,8,2,32,128]{4,3,2,1,0:T(8,128)(2,1)S(1)} %bitcast.24, bf16[2,8,16,8,128]{4,3,2,1,0:T(8,128)(2,1)S(1)} %bitcast.25), custom_call_target="tpu_custom_call" | custom-call | tf_op jit(solution)/shard_map/corner_turn/pallas_call | solution.py:286
  77.9 1.1 %azimuth_correlate.1 = f32[2,32,4096]{2,1,0:T(8,128)S(1)} custom-call(bf16[2,2,16,32,128]{4,3,2,1,0:T(8,128)(2,1)S(1)} %get-tuple-element.7.turned_ref, bf16[2,512]{1,0:T(2,128)(2,1)S(1)} %reshape.33.row_ref), custom_call_target="tpu_custom_call" | custom-call | tf_op jit(solution)/shard_map/azimuth_correlate/pallas_call | solution.py:306
  79.0 1.8 %copy.10 = f32[1,32,2,4096]{3,2,1,0:T(2,128)} copy(f32[1,32,2,4096]{3,1,2,0:T(8,128)S(1)} %bitcast.23) | data formatting | bytes 2097152 | tf_op jit(solution)/shard_map/broadcast_in_dim | solution.py:315
  (6 shorter events, 0.1 us)
Async XLA Ops:
  0.0 3.3 %copy-start = (s32[4,128]{1,0:T(4,128)S(1)}, s32[4,128]{1,0:T(4,128)}, u32[]{:S(2)}) copy-start(s32[4,128]{1,0:T(4,128)} %param.8) | copy-start | bytes 6148
  0.0 3.3 %copy-start.2 = (bf16[2,1024]{1,0:T(2,128)(2,1)S(1)}, bf16[2,1024]{1,0:T(2,128)(2,1)}, u32[]{:S(2)}) copy-start(bf16[2,1024]{1,0:T(2,128)(2,1)} %param.6) | copy-start | bytes 12292
  0.0 3.3 %copy-start.1 = (bf16[8,2,512]{2,1,0:T(2,128)(2,1)S(1)}, bf16[8,2,512]{2,1,0:T(2,128)(2,1)}, u32[]{:S(2)}) copy-start(bf16[8,2,512]{2,1,0:T(2,128)(2,1)} %param.7) | copy-start | bytes 49156
  1.9 2.7 %collective-permute-start = (bf16[2,32,3072]{2,1,0:T(8,128)(2,1)S(1)}, bf16[2,32,3072]{2,1,0:T(8,128)(2,1)S(1)}, u32[]{:S(2)}, u32[]{:S(2)}) collective-permute-start(bf16[2,32,3072]{2,1,0:T(8,128)(2,1)S(1)} %slice.4), channel_id=1, source_target_pairs={{1,0},{2,1},{5,4},{6,5},{9,8},{10,9},{13,12},{14,13},{17,16},{18,1... | collective-permute-start | bytes 1179656 | tf_op jit(solution)/shard_map/ppermute | solution.py:268

commit v2 on v1

v2 whole, which is shorter than its diff:
```python
import functools

import jax
import jax.numpy as jnp
from jax import lax
from jax.experimental import pallas as pl
from jax.experimental.pallas import tpu as pltpu
from jax.sharding import PartitionSpec as P

MESH = pl.DeviceIdType.MESH
BF16 = jnp.bfloat16
F32 = jnp.float32
NT = (((1,), (1,)), ((), ()))
SPAN = 1664
HALO = 3072
REACH = 5248
VMEM = pl.BlockSpec(memory_space=pltpu.VMEM)
SMEM = pl.BlockSpec(memory_space=pltpu.SMEM)
ANY = pl.BlockSpec(memory_space=pl.ANY)


def prepare_kernel(start_ref, chirp_ref, planar_ref, taps_ref, window_ref, local_ref, halo_ref, tail, head):
    start = start_ref[0]
    base = pl.multiple_of((start // 128) * 128, 128)
    taps_ref[...] = jnp.zeros_like(taps_ref)
    for part in range(2):
        row = jnp.concatenate([chirp_ref[part : part + 1, :], jnp.zeros((1, 256), F32)], axis=1)
        row = pltpu.roll(jnp.broadcast_to(row, (8, 1280)), start - base, 1)[:1]
        wide = pltpu.roll(jnp.broadcast_to(row, (128, 1280)), 0, 1, stride=1, stride_axis=0)
        wide = wide.astype(BF16)
        for y in range(4):
            for g in range(4):
                r0 = part * 128 + g * 32
                taps_ref[y, r0 : r0 + 32, 128 * g : 128 * g + 1280] = wide[32 * y : 32 * y + 32, :]
    tail[:, :, :4096] = planar_ref[:, :, 4096:]
    tail[:, :, 4096:] = jnp.zeros((2, 32, HALO), BF16)
    head[:, :, :1920] = jnp.zeros((2, 32, 1920), BF16)
    head[:, :, 1920:] = planar_ref[:, :, :HALO]
    window_ref[...] = planar_ref[:, :, pl.ds(base, REACH)]
    local_ref[...] = tail[:, :, pl.ds(base, REACH)]
    halo_ref[...] = head[:, :, pl.ds(base, HALO)]


def turn_kernel(
    taps_ref, window_ref, local_ref, halo_ref, refs_ref, pick_ref, turned_ref, row_ref,
    hb, w1, yb, xr, zs, ga, rs, rz, sh, rh, sx, rx, sz, rzs, srow, rrow, szrow, rzrow,
):
    pa = lax.axis_index("pa")
    sa = lax.axis_index("sa")
    xlo, z, y = pa // 64, (pa // 4) % 16, pa % 4
    xhi, core = sa // 2, sa % 2
    here = xlo * 16 + z
    across = jnp.where(xhi == 0, xlo, 1 - xlo)
    is_source = xhi == 0

    def order(jj, t):
        return (z // 4 + t) % 4 if jj == 0 else (z // 4 + 4 - t) % 4

    barrier = pltpu.get_barrier_semaphore()

    def greet_source(i, carry):
        dev = (across * 16 + z) * 4 + i

        @pl.when(jnp.logical_or(dev != pa, xhi != sa))
        def _():
            pl.semaphore_signal(barrier, inc=1, device_id=(dev, xhi), device_id_type=MESH)

        return carry

    lax.fori_loop(0, 4, greet_source, 0)

    @pl.when(sa != 0)
    def _():
        def greet_y(i, carry):
            dev = here * 4 + (y + i) % 4
            pl.semaphore_signal(barrier, inc=1, device_id=(dev, sa), device_id_type=MESH)
            return carry

        lax.fori_loop(1, 4, greet_y, 0)

    def greet_line(i, carry):
        dev = ((here + i) % 32) * 4 + y
        pl.semaphore_signal(barrier, inc=1, device_id=(dev, sa), device_id_type=MESH)
        return carry

    lax.fori_loop(1, 32, greet_line, 0)

    @pl.when(sa < 2)
    def _():
        pl.semaphore_signal(barrier, inc=1, device_id=(pa, sa + 1), device_id_type=MESH)

    @pl.when(sa == 0)
    def _():
        pl.semaphore_wait(barrier, 38)

    @pl.when(sa == 1)
    def _():
        pl.semaphore_wait(barrier, 43)

    @pl.when(sa == 2)
    def _():
        pl.semaphore_wait(barrier, 35)

    @pl.when(sa == 3)
    def _():
        pl.semaphore_wait(barrier, 34)

    @pl.when(jnp.logical_or(sa == 1, sa == 2))
    def _():
        pltpu.make_async_remote_copy(
            halo_ref, hb, sh, rh,
            device_id=(pa, sa - 1), device_id_type=MESH,
        ).start()

    def row_send(i, carry):
        dev = here * 4 + (y + i) % 4
        pltpu.make_async_remote_copy(
            refs_ref, ga.at[y], srow, rrow, device_id=(dev, sa), device_id_type=MESH
        ).start()
        return carry

    lax.fori_loop(1, 4, row_send, 0)
    pltpu.make_async_copy(refs_ref, ga.at[y], rrow).start()

    eye = (
        lax.broadcasted_iota(jnp.int32, (128, 128), 0) == lax.broadcasted_iota(jnp.int32, (128, 128), 1)
    ).astype(BF16)

    def correlate(window, jj, k):
        pieces = []
        for c in range(2):
            for x in range(2):
                off = pl.multiple_of(x * 2048 + k * 512, 128)
                pieces.append(window[c, :, pl.ds(off, SPAN)])
        lhs = jnp.concatenate(pieces, axis=0)
        for dest in range(4):
            got = lax.dot_general(lhs, taps_ref[dest], NT, preferred_element_type=F32)
            real = (got[:64, :128] + got[64:, 128:]).astype(BF16)
            imag = (got[64:, :128] - got[:64, 128:]).astype(BF16)
            slot = (jj * 4 + k) * 4 + dest
            for x in range(2):
                yb[slot, x, 0] = real[32 * x : 32 * x + 32]
                yb[slot, x, 1] = imag[32 * x : 32 * x + 32]

        def send(i, carry):
            dest = (y + i) % 4
            dev = ((jnp.where(core == 0, xlo, 1 - xlo)) * 16 + z) * 4 + dest
            target = 2 * core + jj
            there = jnp.logical_or(dev != pa, target != sa)
            slot = (jj * 4 + k) * 4 + dest

            @pl.when(there)
            def _():
                pltpu.make_async_remote_copy(
                    yb.at[slot], xr.at[k, :, :, y], sx, rx.at[k],
                    device_id=(dev, target), device_id_type=MESH,
                ).start()

            @pl.when(jnp.logical_not(there))
            def _():
                pltpu.make_async_copy(yb.at[slot], xr.at[k, :, :, y], rx.at[k]).start()

            return carry

        lax.fori_loop(0, 4, send, 0)

    def pass_on(k):
        pltpu.make_async_copy(xr.at[k], xr.at[k], rx.at[k]).wait()
        for x in range(2):
            pulses = xr[k, x].reshape(256, 128)
            flipped = lax.dot_general(eye, pulses, NT, preferred_element_type=F32).astype(BF16)
            for g in range(4):
                for c in range(2):
                    zs[16 * x + 4 * k + g, c] = flipped[32 * g : 32 * g + 32, 128 * c : 128 * c + 128]

        def send(i, carry):
            dest = (i // 4) * 16 + 4 * k + i % 4

            @pl.when(dest != here)
            def _():
                pltpu.make_async_remote_copy(
                    zs.at[dest], turned_ref.at[:, across * 16 + z], sz, rzs,
                    device_id=(dest * 4 + y, sa), device_id_type=MESH,
                ).start()

            @pl.when(dest == here)
            def _():
                pltpu.make_async_copy(zs.at[dest], turned_ref.at[:, across * 16 + z], rzs).start()

            return carry

        lax.fori_loop(0, 8, send, 0)

    @pl.when(is_source)
    def _():
        def first(t, carry):
            correlate(window_ref, 0, order(0, t))

            @pl.when(jnp.logical_and(sa == 0, t >= 1))
            def _():
                pass_on(order(0, t - 1))

            return carry

        lax.fori_loop(0, 4, first, 0)
        pltpu.make_async_copy(hb, hb, rh).wait()
        w1[:, :, : REACH - HALO] = local_ref[:, :, : REACH - HALO]
        w1[:, :, REACH - HALO :] = local_ref[:, :, REACH - HALO :] + hb[...]

    pltpu.make_async_copy(ga, ga, rrow).wait()
    wanted = jnp.dot(pick_ref[...], ga[...].reshape(64, 512), preferred_element_type=F32)
    for dest in range(32):
        rs[dest] = wanted[2 * dest : 2 * dest + 2]

    def row_pass(i, carry):
        dest = (here + i) % 32
        pltpu.make_async_remote_copy(
            rs.at[dest], rz.at[here], szrow, rzrow, device_id=(dest * 4 + y, sa), device_id_type=MESH
        ).start()
        return carry

    lax.fori_loop(1, 32, row_pass, 0)
    pltpu.make_async_copy(rs.at[here], rz.at[here], rzrow).start()

    @pl.when(is_source)
    def _():
        def second(t, carry):
            correlate(w1, 1, order(1, t))

            @pl.when(jnp.logical_or(jnp.logical_and(sa == 0, t == 0), jnp.logical_and(sa == 1, t >= 1)))
            def _():
                pass_on(jnp.where(sa == 0, order(0, 3), order(1, t - 1)))

            return carry

        lax.fori_loop(0, 4, second, 0)

    def rest(t, carry):
        pass_on(jnp.where(core == 0, order(0, t), order(1, t)))
        return carry

    lax.fori_loop(jnp.where(sa == 0, 4, jnp.where(sa == 1, 3, 0)), 4, rest, 0)

    pltpu.make_async_copy(rz, rz, rzrow).wait()
    row_ref[...] = jnp.sum(rz[...], axis=0)

    pltpu.make_async_copy(turned_ref, turned_ref, rzs).wait()
    pltpu.make_async_copy(zs.at[pl.ds(0, 31)], zs.at[pl.ds(0, 31)], sz).wait()
    pltpu.make_async_copy(rs.at[pl.ds(0, 31)], rs.at[pl.ds(0, 31)], szrow).wait()
    pltpu.make_async_copy(ga.at[pl.ds(0, 3)], ga.at[pl.ds(0, 3)], srow).wait()

    @pl.when(jnp.logical_or(sa == 1, sa == 2))
    def _():
        pltpu.make_async_copy(halo_ref, halo_ref, sh).wait()

    @pl.when(sa == 0)
    def _():
        pltpu.make_async_copy(yb.at[pl.ds(0, 28)], yb.at[pl.ds(0, 28)], sx).wait()

    @pl.when(sa == 1)
    def _():
        pltpu.make_async_copy(yb, yb, sx).wait()


def azimuth_kernel(turned_ref, row_ref, out_ref, lhs, taps):
    zeros = jnp.zeros((32, 256), BF16)
    for c in range(2):
        lhs[c, 0] = zeros
        lhs[c, 17] = zeros
        for block in range(16):
            for half in range(2):
                tile = turned_ref[c, 2 * block + half]
                lhs[c, block + 1, :, 128 * half : 128 * half + 128] = tile
    for part in range(2):
        row = jnp.concatenate([row_ref[part : part + 1, :], jnp.zeros((1, 512), F32)], axis=1)
        wide = pltpu.roll(jnp.broadcast_to(row, (256, 1024)), 0, 1, stride=1, stride_axis=0)
        taps[256 * part : 256 * part + 256, :] = wide[:, :768].astype(BF16)
    got = []
    for c in range(2):
        total = None
        for o in range(3):
            rows = lhs[c, o : o + 16].reshape(512, 256)
            piece = lax.dot_general(rows, taps[:, 256 * o : 256 * o + 256], NT, preferred_element_type=F32)
            total = piece if total is None else total + piece
        got.append(total)
    real = got[0][:, :256] + got[1][:, 256:]
    imag = got[1][:, :256] - got[0][:, 256:]
    for block in range(16):
        out_ref[0, :, 256 * block : 256 * block + 256] = real[32 * block : 32 * block + 32]
        out_ref[1, :, 256 * block : 256 * block + 256] = imag[32 * block : 32 * block + 32]


def params(**more):
    return pltpu.CompilerParams(vmem_limit_bytes=48 << 20, **more)


def on_device(raw_echo, chirp_replica, azimuth_refs, migration_index, window_start):
    pa = lax.axis_index("pa")
    sa = lax.axis_index("sa")
    planar = jnp.transpose(raw_echo, (1, 0, 2))
    taps, window, local, halo = pl.pallas_call(
        prepare_kernel,
        out_shape=(
            jax.ShapeDtypeStruct((4, 256, SPAN), BF16),
            jax.ShapeDtypeStruct((2, 32, REACH), BF16),
            jax.ShapeDtypeStruct((2, 32, REACH), BF16),
            jax.ShapeDtypeStruct((2, 32, HALO), BF16),
        ),
        in_specs=[SMEM, VMEM, VMEM],
        out_specs=(VMEM,) * 4,
        scratch_shapes=[pltpu.VMEM((2, 32, 7168), BF16), pltpu.VMEM((2, 32, 4992), BF16)],
        compiler_params=params(),
        name="prepare",
    )(window_start, chirp_replica.astype(F32), planar)

    index = lax.dynamic_slice_in_dim(migration_index, sa, 1, 0).reshape(32, 4)
    index = lax.dynamic_slice_in_dim(index, pa % 4, 1, 1)[:, :, None]
    slot = 2 * (index % 32) + jnp.arange(2)[None, :, None]
    picked = jnp.logical_and(index // 32 == pa // 4, slot == jnp.arange(64)[None, None, :])
    pick = picked.reshape(64, 64).astype(BF16)

    dma = pltpu.SemaphoreType.DMA
    turned, row = pl.pallas_call(
        turn_kernel,
        out_shape=(
            jax.ShapeDtypeStruct((2, 32, 32, 128), BF16),
            jax.ShapeDtypeStruct((2, 512), F32),
        ),
        in_specs=[VMEM] * 6,
        out_specs=(ANY, VMEM),
        scratch_shapes=[
            pltpu.VMEM((2, 32, HALO), BF16),
            pltpu.VMEM((2, 32, REACH), BF16),
            pltpu.VMEM((32, 2, 2, 32, 128), BF16),
            pltpu.VMEM((4, 2, 2, 4, 32, 128), BF16),
            pltpu.VMEM((32, 2, 32, 128), BF16),
            pltpu.VMEM((4, 16, 512), BF16),
            pltpu.VMEM((32, 2, 512), F32),
            pltpu.VMEM((32, 2, 512), F32),
            dma, dma, dma, dma((4,)), dma, dma, dma, dma, dma, dma,
        ],
        compiler_params=params(collective_id=0, has_side_effects=True),
        name="corner_turn",
    )(taps, window, local, halo, azimuth_refs.reshape(16, 512), pick)

    image = pl.pallas_call(
        azimuth_kernel,
        out_shape=jax.ShapeDtypeStruct((2, 32, 4096), F32),
        in_specs=[VMEM, VMEM],
        out_specs=VMEM,
        scratch_shapes=[pltpu.VMEM((2, 18, 32, 256), BF16), pltpu.VMEM((512, 768), BF16)],
        compiler_params=params(),
        name="azimuth_correlate",
    )(turned, row)
    return jnp.transpose(image, (1, 0, 2))[None]


def solution(mesh):
    placed = (P("pa", None, "sa"), P(), P("pa", None, None), P(), P())
    return jax.shard_map(
        on_device, mesh=mesh, in_specs=placed, out_specs=P("sa", "pa", None, None), check_vma=False
    )
```

time: 80.9 us -> 70.7 us (0.87)
  the two profiles are of different devices: /device:TPU:5 before, /device:TPU:35 now
where the time goes in v2:
time: 70.7 us; the launch traced here: 70.3 us
  Pallas kernels  58.1 us (82%)
  local copies, waits for them, and re-layouts  10.5 us (15%)
  other arithmetic  0.88 us (1%)
  between operations  0.79 us (1%)
    pallas_call x1, Pallas kernels, on_device(): pl.pallas_call(turn_kernel, out_shape=(jax.ShapeDtypeStruct((2, 32, 32, 1...  56.3 us
    unnamed x15, local copies, waits for them, and re-layouts  7.41 us
    broadcast_in_dim x1, local copies, waits for them, and re-layouts, on_device(): return jnp.transpose(image, (1, 0, 2))[None]  1.78 us

profile of v2, /device:TPU:35, one launch (start us, length us, event | category | flops | bytes accessed | tf_op | source)
XLA Modules:
  0.0 70.3 jit_solution(15407353531874070821)
XLA Ops:
  0.0 0.0 copy-start
  0.7 0.7 convert_element_type.6.chirp_ref
  1.4 1.8 %copy.11 = bf16[32,2,8192]{2,0,1:T(8,128)(2,1)S(1)} copy(bf16[32,2,8192]{2,1,0:T(2,128)(2,1)} %param.5) | data formatting | bytes 2097152 | tf_op args[0]
  3.2 0.7 prepare.1
  3.9 0.0 copy-start.1
  3.9 0.8 %copy-done.1 = bf16[2,32,5248]{2,1,0:T(8,128)(2,1)} copy-done((bf16[2,32,5248]{2,1,0:T(8,128)(2,1)}, bf16[2,32,5248]{2,1,0:T(8,128)(2,1)S(1)}, u32[]{:S(2)}) %copy-start.1) | copy-done | bytes 671768
  4.7 0.0 copy-start.3
  4.7 0.9 %copy-done.3 = bf16[2,32,5248]{2,1,0:T(8,128)(2,1)} copy-done((bf16[2,32,5248]{2,1,0:T(8,128)(2,1)}, bf16[2,32,5248]{2,1,0:T(8,128)(2,1)S(1)}, u32[]{:S(2)}) %copy-start.3) | copy-done | bytes 671768
  5.6 0.0 copy-start.5
  5.6 0.7 %copy-done.5 = bf16[2,32,3072]{2,1,0:T(8,128)(2,1)} copy-done((bf16[2,32,3072]{2,1,0:T(8,128)(2,1)}, bf16[2,32,3072]{2,1,0:T(8,128)(2,1)S(1)}, u32[]{:S(2)}) %copy-start.5) | copy-done | bytes 393240
  6.3 0.7 %reshape.123.refs_ref = bf16[16,512]{1,0:T(8,128)(2,1)S(1)} reshape(bf16[8,2,512]{2,1,0:T(2,128)(2,1)} %param.7) | data formatting | bytes 32768 | tf_op jit(solution)/shard_map/reshape | solution.py:344
  7.0 0.0 copy-done
  7.1 0.1 reshape.124
  7.2 0.2 dynamic-slice_reduce_fusion
  7.4 0.1 iota_add_fusion
  7.5 0.1 add.56
  7.6 0.1 and.56
  7.7 0.1 and.57
  7.8 0.1 fusion.1.pick_ref
  7.9 0.0 copy-start.2
  7.9 1.1 %copy-done.2 = bf16[2,32,5248]{2,1,0:T(8,128)(2,1)S(1)} copy-done((bf16[2,32,5248]{2,1,0:T(8,128)(2,1)S(1)}, bf16[2,32,5248]{2,1,0:T(8,128)(2,1)}, u32[]{:S(2)}) %copy-start.2) | copy-done | bytes 671768
  9.0 0.0 copy-start.4
  9.0 1.1 %copy-done.4 = bf16[2,32,5248]{2,1,0:T(8,128)(2,1)S(1)} copy-done((bf16[2,32,5248]{2,1,0:T(8,128)(2,1)S(1)}, bf16[2,32,5248]{2,1,0:T(8,128)(2,1)}, u32[]{:S(2)}) %copy-start.4) | copy-done | bytes 671768
  10.1 0.0 copy-start.6
  10.1 1.0 %copy-done.6 = bf16[2,32,3072]{2,1,0:T(8,128)(2,1)S(1)} copy-done((bf16[2,32,3072]{2,1,0:T(8,128)(2,1)S(1)}, bf16[2,32,3072]{2,1,0:T(8,128)(2,1)}, u32[]{:S(2)}) %copy-start.6) | copy-done | bytes 393240
  11.1 56.3 %corner_turn.1 = (bf16[2,32,32,128]{3,2,1,0:T(8,128)(2,1)S(1)}, f32[2,512]{1,0:T(2,128)S(1)}) custom-call(bf16[4,256,1664]{2,1,0:T(8,128)(2,1)S(1)} %get-tuple-element.11.taps_ref, bf16[2,32,5248]{2,1,0:T(8,128)(2,1)S(1)} %copy-done.2, bf16[2,32,5248]{2,1,0:T(8,128)(2,1)S(1)} %copy-done.4, bf16[2,32,3072]{2,1,0:T(8,128)(2,1)S(1)} %copy-done.6, ...), custom_call_target="tpu_custom_call" | custom-call | tf_op jit(solution)/shard_map/corner_turn/pallas_call | solution.py:323
  67.4 1.1 %azimuth_correlate.1 = f32[2,32,4096]{2,1,0:T(8,128)S(1)} custom-call(bf16[2,32,32,128]{3,2,1,0:T(8,128)(2,1)S(1)} %get-tuple-element.15.turned_ref, f32[2,512]{1,0:T(2,128)S(1)} %get-tuple-element.16.row_ref), custom_call_target="tpu_custom_call" | custom-call | tf_op jit(solution)/shard_map/azimuth_correlate/pallas_call | solution.py:346
  68.5 1.8 %copy.9 = f32[1,32,2,4096]{3,2,1,0:T(2,128)} copy(f32[1,32,2,4096]{3,1,2,0:T(8,128)S(1)} %bitcast.7) | data formatting | bytes 2097152 | tf_op jit(solution)/shard_map/broadcast_in_dim | solution.py:355
  (3 shorter events, 0.0 us)
Async XLA Ops:
  0.0 7.0 %copy-start = (s32[4,128]{1,0:T(4,128)S(1)}, s32[4,128]{1,0:T(4,128)}, u32[]{:S(2)}) copy-start(s32[4,128]{1,0:T(4,128)} %param.8) | copy-start | bytes 6148
  3.9 0.8 %copy-start.1 = (bf16[2,32,5248]{2,1,0:T(8,128)(2,1)}, bf16[2,32,5248]{2,1,0:T(8,128)(2,1)S(1)}, u32[]{:S(2)}) copy-start(bf16[2,32,5248]{2,1,0:T(8,128)(2,1)S(1)} %get-tuple-element.12.window_ref) | copy-start | bytes 2015236
  4.7 0.9 %copy-start.3 = (bf16[2,32,5248]{2,1,0:T(8,128)(2,1)}, bf16[2,32,5248]{2,1,0:T(8,128)(2,1)S(1)}, u32[]{:S(2)}) copy-start(bf16[2,32,5248]{2,1,0:T(8,128)(2,1)S(1)} %get-tuple-element.13.local_ref) | copy-start | bytes 2015236
  5.6 0.7 %copy-start.5 = (bf16[2,32,3072]{2,1,0:T(8,128)(2,1)}, bf16[2,32,3072]{2,1,0:T(8,128)(2,1)S(1)}, u32[]{:S(2)}) copy-start(bf16[2,32,3072]{2,1,0:T(8,128)(2,1)S(1)} %get-tuple-element.14.halo_ref) | copy-start | bytes 1179652
  7.9 1.1 %copy-start.2 = (bf16[2,32,5248]{2,1,0:T(8,128)(2,1)S(1)}, bf16[2,32,5248]{2,1,0:T(8,128)(2,1)}, u32[]{:S(2)}) copy-start(bf16[2,32,5248]{2,1,0:T(8,128)(2,1)} %copy-done.1) | copy-start | bytes 2015236
  9.0 1.1 %copy-start.4 = (bf16[2,32,5248]{2,1,0:T(8,128)(2,1)S(1)}, bf16[2,32,5248]{2,1,0:T(8,128)(2,1)}, u32[]{:S(2)}) copy-start(bf16[2,32,5248]{2,1,0:T(8,128)(2,1)} %copy-done.3) | copy-start | bytes 2015236
  10.1 1.0 %copy-start.6 = (bf16[2,32,3072]{2,1,0:T(8,128)(2,1)S(1)}, bf16[2,32,3072]{2,1,0:T(8,128)(2,1)}, u32[]{:S(2)}) copy-start(bf16[2,32,3072]{2,1,0:T(8,128)(2,1)} %copy-done.5) | copy-start | bytes 1179652

commit v3 on v2

--- a/solution.py
+++ b/solution.py
@@ -19,12 +19,23 @@
 ANY = pl.BlockSpec(memory_space=pl.ANY)
 
 
-def prepare_kernel(start_ref, chirp_ref, planar_ref, taps_ref, window_ref, local_ref, halo_ref, tail, head):
+def prepare_kernel(
+    start_ref, index_ref, chirp_ref, planar_ref, taps_ref, window_ref, local_ref, halo_ref, pick_ref, tail, head
+):
+    pa = lax.axis_index("pa")
+    sa = lax.axis_index("sa")
+    line = lax.broadcasted_iota(jnp.int32, (64, 64), 0)
+    code = jnp.full((64, 64), -2, jnp.int32)
+    for dest in range(32):
+        index = index_ref[sa, 4 * dest + pa % 4]
+        code = jnp.where(line // 2 == dest, jnp.where(index // 32 == pa // 4, 2 * (index % 32), -2), code)
+    pick_ref[...] = (lax.broadcasted_iota(jnp.int32, (64, 64), 1) == code + line % 2).astype(F32).astype(BF16)
+
     start = start_ref[0]
     base = pl.multiple_of((start // 128) * 128, 128)
     taps_ref[...] = jnp.zeros_like(taps_ref)
     for part in range(2):
-        row = jnp.concatenate([chirp_ref[part : part + 1, :], jnp.zeros((1, 256), F32)], axis=1)
+        row = jnp.concatenate([chirp_ref[part : part + 1, :].astype(F32), jnp.zeros((1, 256), F32)], axis=1)
         row = pltpu.roll(jnp.broadcast_to(row, (8, 1280)), start - base, 1)[:1]
         wide = pltpu.roll(jnp.broadcast_to(row, (128, 1280)), 0, 1, stride=1, stride_axis=0)
         wide = wide.astype(BF16)
@@ -53,9 +64,6 @@
     across = jnp.where(xhi == 0, xlo, 1 - xlo)
     is_source = xhi == 0
 
-    def order(jj, t):
-        return (z // 4 + t) % 4 if jj == 0 else (z // 4 + 4 - t) % 4
-
     barrier = pltpu.get_barrier_semaphore()
 
     def greet_source(i, carry):
@@ -126,24 +134,28 @@
         lax.broadcasted_iota(jnp.int32, (128, 128), 0) == lax.broadcasted_iota(jnp.int32, (128, 128), 1)
     ).astype(BF16)
 
-    def correlate(window, jj, k):
+    def correlate(window, jj, t):
+        first = (z // 4 + t) % 2
         pieces = []
         for c in range(2):
-            for x in range(2):
-                off = pl.multiple_of(x * 2048 + k * 512, 128)
-                pieces.append(window[c, :, pl.ds(off, SPAN)])
+            for kk in range(2):
+                for x in range(2):
+                    off = pl.multiple_of(x * 2048 + (first + 2 * kk) * 512, 128)
+                    pieces.append(window[c, :, pl.ds(off, SPAN)])
         lhs = jnp.concatenate(pieces, axis=0)
         for dest in range(4):
             got = lax.dot_general(lhs, taps_ref[dest], NT, preferred_element_type=F32)
-            real = (got[:64, :128] + got[64:, 128:]).astype(BF16)
-            imag = (got[64:, :128] - got[:64, 128:]).astype(BF16)
-            slot = (jj * 4 + k) * 4 + dest
-            for x in range(2):
-                yb[slot, x, 0] = real[32 * x : 32 * x + 32]
-                yb[slot, x, 1] = imag[32 * x : 32 * x + 32]
+            real = (got[:128, :128] + got[128:, 128:]).astype(BF16)
+            imag = (got[128:, :128] - got[:128, 128:]).astype(BF16)
+            for kk in range(2):
+                slot = (jj * 4 + first + 2 * kk) * 4 + dest
+                for x in range(2):
+                    r0 = 64 * kk + 32 * x
+                    yb[slot, x, 0] = real[r0 : r0 + 32]
+                    yb[slot, x, 1] = imag[r0 : r0 + 32]
 
         def send(i, carry):
-            dest = (y + i) % 4
+            k, dest = first + 2 * (i // 4), (y + i) % 4
             dev = ((jnp.where(core == 0, xlo, 1 - xlo)) * 16 + z) * 4 + dest
             target = 2 * core + jj
             there = jnp.logical_or(dev != pa, target != sa)
@@ -162,7 +174,7 @@
 
             return carry
 
-        lax.fori_loop(0, 4, send, 0)
+        lax.fori_loop(0, 8, send, 0)
 
     def pass_on(k):
         pltpu.make_async_copy(xr.at[k], xr.at[k], rx.at[k]).wait()
@@ -193,19 +205,20 @@
 
     @pl.when(is_source)
     def _():
-        def first(t, carry):
-            correlate(window_ref, 0, order(0, t))
-
-            @pl.when(jnp.logical_and(sa == 0, t >= 1))
-            def _():
-                pass_on(order(0, t - 1))
-
-            return carry
-
-        lax.fori_loop(0, 4, first, 0)
+        def first_half(t, carry):
+            correlate(window_ref, 0, t)
+            return carry
+
+        lax.fori_loop(0, 2, first_half, 0)
         pltpu.make_async_copy(hb, hb, rh).wait()
         w1[:, :, : REACH - HALO] = local_ref[:, :, : REACH - HALO]
         w1[:, :, REACH - HALO :] = local_ref[:, :, REACH - HALO :] + hb[...]
+
+        def second_half(t, carry):
+            correlate(w1, 1, t)
+            return carry
+
+        lax.fori_loop(0, 2, second_half, 0)
 
     pltpu.make_async_copy(ga, ga, rrow).wait()
     wanted = jnp.dot(pick_ref[...], ga[...].reshape(64, 512), preferred_element_type=F32)
@@ -222,24 +235,11 @@
     lax.fori_loop(1, 32, row_pass, 0)
     pltpu.make_async_copy(rs.at[here], rz.at[here], rzrow).start()
 
-    @pl.when(is_source)
-    def _():
-        def second(t, carry):
-            correlate(w1, 1, order(1, t))
-
-            @pl.when(jnp.logical_or(jnp.logical_and(sa == 0, t == 0), jnp.logical_and(sa == 1, t >= 1)))
-            def _():
-                pass_on(jnp.where(sa == 0, order(0, 3), order(1, t - 1)))
-
-            return carry
-
-        lax.fori_loop(0, 4, second, 0)
-
     def rest(t, carry):
-        pass_on(jnp.where(core == 0, order(0, t), order(1, t)))
-        return carry
-
-    lax.fori_loop(jnp.where(sa == 0, 4, jnp.where(sa == 1, 3, 0)), 4, rest, 0)
+        pass_on((z // 4 + t // 2) % 2 + 2 * (t % 2))
+        return carry
+
+    lax.fori_loop(0, 4, rest, 0)
 
     pltpu.make_async_copy(rz, rz, rzrow).wait()
     row_ref[...] = jnp.sum(rz[...], axis=0)
@@ -291,33 +291,26 @@
 
 
 def params(**more):
-    return pltpu.CompilerParams(vmem_limit_bytes=48 << 20, **more)
+    return pltpu.CompilerParams(vmem_limit_bytes=20 << 20, **more)
 
 
 def on_device(raw_echo, chirp_replica, azimuth_refs, migration_index, window_start):
-    pa = lax.axis_index("pa")
-    sa = lax.axis_index("sa")
     planar = jnp.transpose(raw_echo, (1, 0, 2))
-    taps, window, local, halo = pl.pallas_call(
+    taps, window, local, halo, pick = pl.pallas_call(
         prepare_kernel,
         out_shape=(
             jax.ShapeDtypeStruct((4, 256, SPAN), BF16),
             jax.ShapeDtypeStruct((2, 32, REACH), BF16),
             jax.ShapeDtypeStruct((2, 32, REACH), BF16),
             jax.ShapeDtypeStruct((2, 32, HALO), BF16),
+            jax.ShapeDtypeStruct((64, 64), BF16),
         ),
-        in_specs=[SMEM, VMEM, VMEM],
-        out_specs=(VMEM,) * 4,
+        in_specs=[SMEM, SMEM, VMEM, VMEM],
+        out_specs=(VMEM,) * 5,
         scratch_shapes=[pltpu.VMEM((2, 32, 7168), BF16), pltpu.VMEM((2, 32, 4992), BF16)],
         compiler_params=params(),
         name="prepare",
-    )(window_start, chirp_replica.astype(F32), planar)
-
-    index = lax.dynamic_slice_in_dim(migration_index, sa, 1, 0).reshape(32, 4)
-    index = lax.dynamic_slice_in_dim(index, pa % 4, 1, 1)[:, :, None]
-    slot = 2 * (index % 32) + jnp.arange(2)[None, :, None]
-    picked = jnp.logical_and(index // 32 == pa // 4, slot == jnp.arange(64)[None, None, :])
-    pick = picked.reshape(64, 64).astype(BF16)
+    )(window_start, migration_index, chirp_replica, planar)
 
     dma = pltpu.SemaphoreType.DMA
     turned, row = pl.pallas_call(
@@ -334,14 +327,14 @@
             pltpu.VMEM((32, 2, 2, 32, 128), BF16),
             pltpu.VMEM((4, 2, 2, 4, 32, 128), BF16),
             pltpu.VMEM((32, 2, 32, 128), BF16),
-            pltpu.VMEM((4, 16, 512), BF16),
+            pltpu.VMEM((4, 8, 2, 512), BF16),
             pltpu.VMEM((32, 2, 512), F32),
             pltpu.VMEM((32, 2, 512), F32),
             dma, dma, dma, dma((4,)), dma, dma, dma, dma, dma, dma,
         ],
         compiler_params=params(collective_id=0, has_side_effects=True),
         name="corner_turn",
-    )(taps, window, local, halo, azimuth_refs.reshape(16, 512), pick)
+    )(taps, window, local, halo, azimuth_refs, pick)
 
     image = pl.pallas_call(
         azimuth_kernel,

time: 70.7 us -> 62.9 us (0.89)
  the two profiles are of different devices: /device:TPU:35 before, /device:TPU:3 now
where the time goes in v3:
time: 62.9 us; the launch traced here: 62.6 us
  Pallas kernels  56.3 us (90%)
  local copies, waits for them, and re-layouts  5.66 us (9%)
  between operations  0.7 us (1%)
    pallas_call x1, Pallas kernels, on_device(): pl.pallas_call(turn_kernel, out_shape=(jax.ShapeDtypeStruct((2, 32, 32, 1...  53.7 us
    unnamed x7, local copies, waits for them, and re-layouts  3.88 us
    broadcast_in_dim x1, local copies, waits for them, and re-layouts, on_device(): return jnp.transpose(image, (1, 0, 2))[None]  1.78 us
    pallas_call x1, Pallas kernels, on_device(): pl.pallas_call(prepare_kernel, out_shape=(jax.ShapeDtypeStruct((4, 256, S...  1.42 us

profile of v3, /device:TPU:3, one launch (start us, length us, event | category | flops | bytes accessed | tf_op | source)
XLA Modules:
  0.0 62.6 jit_solution(9391723838076142883)
XLA Ops:
  0.7 1.8 %copy.9 = bf16[32,2,8192]{2,0,1:T(8,128)(2,1)S(1)} copy(bf16[32,2,8192]{2,1,0:T(2,128)(2,1)} %param.5) | data formatting | bytes 2097152 | tf_op args[0]
  2.5 0.0 copy-start.1
  2.5 0.7 %copy-done.1 = bf16[2,1024]{1,0:T(2,128)(2,1)S(1)} copy-done((bf16[2,1024]{1,0:T(2,128)(2,1)S(1)}, bf16[2,1024]{1,0:T(2,128)(2,1)}, u32[]{:S(2)}) %copy-start.1) | copy-done | bytes 4120
  3.2 0.0 copy-start.2
  3.2 0.7 %copy-done.2 = s32[4,128]{1,0:T(4,128)S(1)} copy-done((s32[4,128]{1,0:T(4,128)S(1)}, s32[4,128]{1,0:T(4,128)}, u32[]{:S(2)}) %copy-start.2) | copy-done | bytes 2072
  3.8 1.4 %prepare.1 = (bf16[4,256,1664]{2,1,0:T(8,128)(2,1)S(1)}, bf16[2,32,5248]{2,1,0:T(8,128)(2,1)S(1)}, bf16[2,32,5248]{2,1,0:T(8,128)(2,1)S(1)}, bf16[2,32,3072]{2,1,0:T(8,128)(2,1)S(1)}, bf16[64,64]{1,0:T(8,128)(2,1)S(1)}) custom-call(s32[1]{0:T(128)S(6)} %copy.10.start_ref, s32[4,128]{1,0:T(4,128)S(1)} %copy-done.2, bf16[2,1024]{1,0:T(2,128)(2,1)S(1)} %copy-done.1, ...), custom_call_target="tpu_custom_call" | custom-call | tf_op jit(solution)/shard_map/prepare/pallas_call | solution.py:299
  5.3 0.0 copy-start
  5.3 0.7 %copy-done = bf16[8,2,512]{2,1,0:T(2,128)(2,1)S(1)} copy-done((bf16[8,2,512]{2,1,0:T(2,128)(2,1)S(1)}, bf16[8,2,512]{2,1,0:T(2,128)(2,1)}, u32[]{:S(2)}) %copy-start) | copy-done | bytes 16408
  6.0 53.7 %corner_turn.1 = (bf16[2,32,32,128]{3,2,1,0:T(8,128)(2,1)S(1)}, f32[2,512]{1,0:T(2,128)S(1)}) custom-call(bf16[4,256,1664]{2,1,0:T(8,128)(2,1)S(1)} %get-tuple-element.12.taps_ref, bf16[2,32,5248]{2,1,0:T(8,128)(2,1)S(1)} %get-tuple-element.13.window_ref, bf16[2,32,5248]{2,1,0:T(8,128)(2,1)S(1)} %get-tuple-element.14.local_ref, ...), custom_call_target="tpu_custom_call" | custom-call | tf_op jit(solution)/shard_map/corner_turn/pallas_call | solution.py:316
  59.7 1.1 %azimuth_correlate.1 = f32[2,32,4096]{2,1,0:T(8,128)S(1)} custom-call(bf16[2,32,32,128]{3,2,1,0:T(8,128)(2,1)S(1)} %get-tuple-element.17.turned_ref, f32[2,512]{1,0:T(2,128)S(1)} %get-tuple-element.18.row_ref), custom_call_target="tpu_custom_call" | custom-call | tf_op jit(solution)/shard_map/azimuth_correlate/pallas_call | solution.py:339
  60.8 1.8 %copy.7 = f32[1,32,2,4096]{3,2,1,0:T(2,128)} copy(f32[1,32,2,4096]{3,1,2,0:T(8,128)S(1)} %bitcast.7) | data formatting | bytes 2097152 | tf_op jit(solution)/shard_map/broadcast_in_dim | solution.py:348
Async XLA Ops:
  2.5 0.7 %copy-start.1 = (bf16[2,1024]{1,0:T(2,128)(2,1)S(1)}, bf16[2,1024]{1,0:T(2,128)(2,1)}, u32[]{:S(2)}) copy-start(bf16[2,1024]{1,0:T(2,128)(2,1)} %chirp_ref.1) | copy-start | bytes 12292
  3.2 0.7 %copy-start.2 = (s32[4,128]{1,0:T(4,128)S(1)}, s32[4,128]{1,0:T(4,128)}, u32[]{:S(2)}) copy-start(s32[4,128]{1,0:T(4,128)} %index_ref.1) | copy-start | bytes 6148
  5.3 0.7 %copy-start = (bf16[8,2,512]{2,1,0:T(2,128)(2,1)S(1)}, bf16[8,2,512]{2,1,0:T(2,128)(2,1)}, u32[]{:S(2)}) copy-start(bf16[8,2,512]{2,1,0:T(2,128)(2,1)} %refs_ref.1) | copy-start | bytes 49156

commit v4 on v3

--- a/solution.py
+++ b/solution.py
@@ -19,42 +19,9 @@
 ANY = pl.BlockSpec(memory_space=pl.ANY)
 
 
-def prepare_kernel(
-    start_ref, index_ref, chirp_ref, planar_ref, taps_ref, window_ref, local_ref, halo_ref, pick_ref, tail, head
-):
-    pa = lax.axis_index("pa")
-    sa = lax.axis_index("sa")
-    line = lax.broadcasted_iota(jnp.int32, (64, 64), 0)
-    code = jnp.full((64, 64), -2, jnp.int32)
-    for dest in range(32):
-        index = index_ref[sa, 4 * dest + pa % 4]
-        code = jnp.where(line // 2 == dest, jnp.where(index // 32 == pa // 4, 2 * (index % 32), -2), code)
-    pick_ref[...] = (lax.broadcasted_iota(jnp.int32, (64, 64), 1) == code + line % 2).astype(F32).astype(BF16)
-
-    start = start_ref[0]
-    base = pl.multiple_of((start // 128) * 128, 128)
-    taps_ref[...] = jnp.zeros_like(taps_ref)
-    for part in range(2):
-        row = jnp.concatenate([chirp_ref[part : part + 1, :].astype(F32), jnp.zeros((1, 256), F32)], axis=1)
-        row = pltpu.roll(jnp.broadcast_to(row, (8, 1280)), start - base, 1)[:1]
-        wide = pltpu.roll(jnp.broadcast_to(row, (128, 1280)), 0, 1, stride=1, stride_axis=0)
-        wide = wide.astype(BF16)
-        for y in range(4):
-            for g in range(4):
-                r0 = part * 128 + g * 32
-                taps_ref[y, r0 : r0 + 32, 128 * g : 128 * g + 1280] = wide[32 * y : 32 * y + 32, :]
-    tail[:, :, :4096] = planar_ref[:, :, 4096:]
-    tail[:, :, 4096:] = jnp.zeros((2, 32, HALO), BF16)
-    head[:, :, :1920] = jnp.zeros((2, 32, 1920), BF16)
-    head[:, :, 1920:] = planar_ref[:, :, :HALO]
-    window_ref[...] = planar_ref[:, :, pl.ds(base, REACH)]
-    local_ref[...] = tail[:, :, pl.ds(base, REACH)]
-    halo_ref[...] = head[:, :, pl.ds(base, HALO)]
-
-
 def turn_kernel(
-    taps_ref, window_ref, local_ref, halo_ref, refs_ref, pick_ref, turned_ref, row_ref,
-    hb, w1, yb, xr, zs, ga, rs, rz, sh, rh, sx, rx, sz, rzs, srow, rrow, szrow, rzrow,
+    start_ref, index_hbm, chirp_hbm, planar_ref, refs_ref, turned_ref, row_ref,
+    index_ref, chirp_ref, taps_ref, pick_ref, w0, w1, halo_ref, hb, yb, xr, zs, ga, rs, rz, sin, sh, rh, sx, rx, sz, rzs, srow, rrow, szrow, rzrow,
 ):
     pa = lax.axis_index("pa")
     sa = lax.axis_index("sa")
@@ -64,6 +31,11 @@
     across = jnp.where(xhi == 0, xlo, 1 - xlo)
     is_source = xhi == 0
 
+    get_index = pltpu.make_async_copy(index_hbm, index_ref, sin.at[0])
+    get_chirp = pltpu.make_async_copy(chirp_hbm, chirp_ref, sin.at[1])
+    get_index.start()
+    get_chirp.start()
+
     barrier = pltpu.get_barrier_semaphore()
 
     def greet_source(i, carry):
@@ -97,42 +69,52 @@
     def _():
         pl.semaphore_signal(barrier, inc=1, device_id=(pa, sa + 1), device_id_type=MESH)
 
-    @pl.when(sa == 0)
-    def _():
-        pl.semaphore_wait(barrier, 38)
-
-    @pl.when(sa == 1)
-    def _():
-        pl.semaphore_wait(barrier, 43)
-
-    @pl.when(sa == 2)
-    def _():
-        pl.semaphore_wait(barrier, 35)
-
-    @pl.when(sa == 3)
-    def _():
-        pl.semaphore_wait(barrier, 34)
+    start = start_ref[0]
+    bits = [jnp.bitwise_and(lax.shift_right_logical(start, bit), 1) == 1 for bit in range(11)]
+
+    def shifted(value):
+        for bit in (10, 9, 8, 7):
+            step = 1 << bit
+            value = jnp.where(bits[bit], value[:, step:], value[:, : value.shape[1] - step])
+        return value
+
+    get_chirp.wait()
+
+    @pl.when(is_source)
+    def _():
+        for part in range(2):
+            row = jnp.concatenate([chirp_ref[part : part + 1, :].astype(F32), jnp.zeros((1, 256), F32)], axis=1)
+            row = jnp.broadcast_to(row, (8, 1280))
+            for bit in range(7):
+                row = jnp.where(bits[bit], pltpu.roll(row, 1 << bit, 1), row)
+            wide = pltpu.roll(jnp.broadcast_to(row[:1], (128, 1280)), 0, 1, stride=1, stride_axis=0)
+            wide = wide.astype(BF16)
+            for dest in range(4):
+                for g in range(4):
+                    r0 = part * 128 + g * 32
+                    if g > 0:
+                        taps_ref[dest, r0 : r0 + 32, : 128 * g] = jnp.zeros((32, 128 * g), BF16)
+                    taps_ref[dest, r0 : r0 + 32, 128 * g : 128 * g + 1280] = wide[32 * dest : 32 * dest + 32, :]
+                    if g < 3:
+                        taps_ref[dest, r0 : r0 + 32, 128 * g + 1280 :] = jnp.zeros((32, 384 - 128 * g), BF16)
+        for c in range(2):
+            for r0 in (0, 16):
+                w0[c, r0 : r0 + 16, :] = shifted(planar_ref[c, r0 : r0 + 16, :7168])
 
     @pl.when(jnp.logical_or(sa == 1, sa == 2))
     def _():
-        pltpu.make_async_remote_copy(
-            halo_ref, hb, sh, rh,
-            device_id=(pa, sa - 1), device_id_type=MESH,
-        ).start()
-
-    def row_send(i, carry):
-        dev = here * 4 + (y + i) % 4
-        pltpu.make_async_remote_copy(
-            refs_ref, ga.at[y], srow, rrow, device_id=(dev, sa), device_id_type=MESH
-        ).start()
-        return carry
-
-    lax.fori_loop(1, 4, row_send, 0)
-    pltpu.make_async_copy(refs_ref, ga.at[y], rrow).start()
-
-    eye = (
-        lax.broadcasted_iota(jnp.int32, (128, 128), 0) == lax.broadcasted_iota(jnp.int32, (128, 128), 1)
-    ).astype(BF16)
+        for c in range(2):
+            for r0 in (0, 16):
+                head = jnp.concatenate([jnp.zeros((16, 1920), BF16), planar_ref[c, r0 : r0 + 16, :HALO]], axis=1)
+                halo_ref[c, r0 : r0 + 16, :] = shifted(head)
+
+    get_index.wait()
+    entry = lax.broadcasted_iota(jnp.int32, (64, 64), 0)
+    code = jnp.full((64, 64), -2, jnp.int32)
+    for dest in range(32):
+        index = index_ref[sa, 4 * dest + y]
+        code = jnp.where(entry // 2 == dest, jnp.where(index // 32 == pa // 4, 2 * (index % 32), -2), code)
+    pick_ref[...] = (lax.broadcasted_iota(jnp.int32, (64, 64), 1) == code + entry % 2).astype(F32).astype(BF16)
 
     def correlate(window, jj, t):
         first = (z // 4 + t) % 2
@@ -154,6 +136,9 @@
                     yb[slot, x, 0] = real[r0 : r0 + 32]
                     yb[slot, x, 1] = imag[r0 : r0 + 32]
 
+    def send_first(jj, t):
+        first = (z // 4 + t) % 2
+
         def send(i, carry):
             k, dest = first + 2 * (i // 4), (y + i) % 4
             dev = ((jnp.where(core == 0, xlo, 1 - xlo)) * 16 + z) * 4 + dest
@@ -175,6 +160,47 @@
             return carry
 
         lax.fori_loop(0, 8, send, 0)
+
+    @pl.when(is_source)
+    def _():
+        correlate(w0, 0, 0)
+
+    @pl.when(sa == 0)
+    def _():
+        pl.semaphore_wait(barrier, 38)
+
+    @pl.when(sa == 1)
+    def _():
+        pl.semaphore_wait(barrier, 43)
+
+    @pl.when(sa == 2)
+    def _():
+        pl.semaphore_wait(barrier, 35)
+
+    @pl.when(sa == 3)
+    def _():
+        pl.semaphore_wait(barrier, 34)
+
+    @pl.when(jnp.logical_or(sa == 1, sa == 2))
+    def _():
+        pltpu.make_async_remote_copy(
+            halo_ref, hb, sh, rh,
+            device_id=(pa, sa - 1), device_id_type=MESH,
+        ).start()
+
+    def row_send(i, carry):
+        dev = here * 4 + (y + i) % 4
+        pltpu.make_async_remote_copy(
+            refs_ref, ga.at[y], srow, rrow, device_id=(dev, sa), device_id_type=MESH
+        ).start()
+        return carry
+
+    lax.fori_loop(1, 4, row_send, 0)
+    pltpu.make_async_copy(refs_ref, ga.at[y], rrow).start()
+
+    eye = (
+        lax.broadcasted_iota(jnp.int32, (128, 128), 0) == lax.broadcasted_iota(jnp.int32, (128, 128), 1)
+    ).astype(BF16)
 
     def pass_on(k):
         pltpu.make_async_copy(xr.at[k], xr.at[k], rx.at[k]).wait()
@@ -205,17 +231,19 @@
 
     @pl.when(is_source)
     def _():
-        def first_half(t, carry):
-            correlate(window_ref, 0, t)
-            return carry
-
-        lax.fori_loop(0, 2, first_half, 0)
+        send_first(0, 0)
+        correlate(w0, 0, 1)
+        send_first(0, 1)
+        for c in range(2):
+            for r0 in (0, 16):
+                tail = jnp.concatenate([planar_ref[c, r0 : r0 + 16, 4096:], jnp.zeros((16, HALO), BF16)], axis=1)
+                w1[c, r0 : r0 + 16, :] = shifted(tail)
         pltpu.make_async_copy(hb, hb, rh).wait()
-        w1[:, :, : REACH - HALO] = local_ref[:, :, : REACH - HALO]
-        w1[:, :, REACH - HALO :] = local_ref[:, :, REACH - HALO :] + hb[...]
+        w1[:, :, REACH - HALO :] = w1[:, :, REACH - HALO :] + hb[...]
 
         def second_half(t, carry):
             correlate(w1, 1, t)
+            send_first(1, t)
             return carry
 
         lax.fori_loop(0, 2, second_half, 0)
@@ -296,22 +324,6 @@
 
 def on_device(raw_echo, chirp_replica, azimuth_refs, migration_index, window_start):
     planar = jnp.transpose(raw_echo, (1, 0, 2))
-    taps, window, local, halo, pick = pl.pallas_call(
-        prepare_kernel,
-        out_shape=(
-            jax.ShapeDtypeStruct((4, 256, SPAN), BF16),
-            jax.ShapeDtypeStruct((2, 32, REACH), BF16),
-            jax.ShapeDtypeStruct((2, 32, REACH), BF16),
-            jax.ShapeDtypeStruct((2, 32, HALO), BF16),
-            jax.ShapeDtypeStruct((64, 64), BF16),
-        ),
-        in_specs=[SMEM, SMEM, VMEM, VMEM],
-        out_specs=(VMEM,) * 5,
-        scratch_shapes=[pltpu.VMEM((2, 32, 7168), BF16), pltpu.VMEM((2, 32, 4992), BF16)],
-        compiler_params=params(),
-        name="prepare",
-    )(window_start, migration_index, chirp_replica, planar)
-
     dma = pltpu.SemaphoreType.DMA
     turned, row = pl.pallas_call(
         turn_kernel,
@@ -319,22 +331,28 @@
             jax.ShapeDtypeStruct((2, 32, 32, 128), BF16),
             jax.ShapeDtypeStruct((2, 512), F32),
         ),
-        in_specs=[VMEM] * 6,
+        in_specs=[SMEM, ANY, ANY, VMEM, ANY],
         out_specs=(ANY, VMEM),
         scratch_shapes=[
+            pltpu.SMEM((4, 128), jnp.int32),
+            pltpu.VMEM((2, 1024), BF16),
+            pltpu.VMEM((4, 256, SPAN), BF16),
+            pltpu.VMEM((64, 64), BF16),
+            pltpu.VMEM((2, 32, REACH), BF16),
+            pltpu.VMEM((2, 32, REACH), BF16),
             pltpu.VMEM((2, 32, HALO), BF16),
-            pltpu.VMEM((2, 32, REACH), BF16),
+            pltpu.VMEM((2, 32, HALO), BF16),
             pltpu.VMEM((32, 2, 2, 32, 128), BF16),
             pltpu.VMEM((4, 2, 2, 4, 32, 128), BF16),
             pltpu.VMEM((32, 2, 32, 128), BF16),
             pltpu.VMEM((4, 8, 2, 512), BF16),
             pltpu.VMEM((32, 2, 512), F32),
             pltpu.VMEM((32, 2, 512), F32),
-            dma, dma, dma, dma((4,)), dma, dma, dma, dma, dma, dma,
+            dma((2,)), dma, dma, dma, dma((4,)), dma, dma, dma, dma, dma, dma,
         ],
         compiler_params=params(collective_id=0, has_side_effects=True),
         name="corner_turn",
-    )(taps, window, local, halo, azimuth_refs, pick)
+    )(window_start, migration_index, chirp_replica, planar, azimuth_refs)
 
     image = pl.pallas_call(
         azimuth_kernel,

time: 62.9 us -> 59.5 us (0.946)
  local copies, waits for them, and re-layouts: 5.66 us -> 3.61 us
  Pallas kernels: 56.3 us -> 55 us
    unnamed x7, local copies, waits for them, and re-layouts: 3.88 us -> 1.83 us
    pallas_call x1 -> x0, Pallas kernels: 1.42 us -> none  [on_device(): pl.pallas_call(prepare_kernel, out_shape=(jax.ShapeDtypeStruct((4, 256, S...]
where the time goes in v4:
time: 59.5 us; the launch traced here: 59.4 us
  Pallas kernels  55 us (92%)
  local copies, waits for them, and re-layouts  3.61 us (6%)
  between operations  0.72 us (1%)
    pallas_call x1, Pallas kernels, on_device(): pl.pallas_call(turn_kernel, out_shape=(jax.ShapeDtypeStruct((2, 32, 32, 1...  53.9 us
    unnamed x7, local copies, waits for them, and re-layouts  1.83 us
    broadcast_in_dim x1, local copies, waits for them, and re-layouts, on_device(): return jnp.transpose(image, (1, 0, 2))[None]  1.78 us

profile of v4, /device:TPU:3, one launch (start us, length us, event | category | flops | bytes accessed | tf_op | source)
XLA Modules:
  0.0 59.4 jit_solution(16600998360183548523)
XLA Ops:
  0.7 0.0 copy-start
  0.7 0.0 copy-start.1
  0.7 0.0 copy-start.2
  0.7 1.8 %copy.9 = bf16[32,2,8192]{2,0,1:T(8,128)(2,1)S(1)} copy(bf16[32,2,8192]{2,1,0:T(2,128)(2,1)} %param.5) | data formatting | bytes 2097152 | tf_op args[0]
  2.5 0.0 copy-done
  2.5 0.0 copy-done.1
  2.5 0.0 copy-done.2
  2.5 53.9 %corner_turn.1 = (bf16[2,32,32,128]{3,2,1,0:T(8,128)(2,1)S(1)}, f32[2,512]{1,0:T(2,128)S(1)}) custom-call(s32[1]{0:T(128)S(6)} %copy.10.start_ref, s32[4,128]{1,0:T(4,128)S(1)} %copy-done.2, bf16[2,1024]{1,0:T(2,128)(2,1)S(1)} %copy-done.1, bf16[2,32,8192]{2,1,0:T(8,128)(2,1)S(1)} %bitcast.6, bf16[8,2,512]{2,1,0:T(2,128)(2,1)S(1)} %copy-done), custom_call_target="tpu_custom_call" | custom-call | tf_op jit(solution)/shard_map/corner_turn/pallas_call | solution.py:328
  56.5 1.1 %azimuth_correlate.1 = f32[2,32,4096]{2,1,0:T(8,128)S(1)} custom-call(bf16[2,32,32,128]{3,2,1,0:T(8,128)(2,1)S(1)} %get-tuple-element.7.turned_ref, f32[2,512]{1,0:T(2,128)S(1)} %get-tuple-element.8.row_ref), custom_call_target="tpu_custom_call" | custom-call | tf_op jit(solution)/shard_map/azimuth_correlate/pallas_call | solution.py:357
  57.6 1.8 %copy.7 = f32[1,32,2,4096]{3,2,1,0:T(2,128)} copy(f32[1,32,2,4096]{3,1,2,0:T(8,128)S(1)} %bitcast.7) | data formatting | bytes 2097152 | tf_op jit(solution)/shard_map/broadcast_in_dim | solution.py:366
Async XLA Ops:
  0.7 1.9 %copy-start = (bf16[8,2,512]{2,1,0:T(2,128)(2,1)S(1)}, bf16[8,2,512]{2,1,0:T(2,128)(2,1)}, u32[]{:S(2)}) copy-start(bf16[8,2,512]{2,1,0:T(2,128)(2,1)} %refs_ref.1) | copy-start | bytes 49156
  0.7 1.9 %copy-start.1 = (bf16[2,1024]{1,0:T(2,128)(2,1)S(1)}, bf16[2,1024]{1,0:T(2,128)(2,1)}, u32[]{:S(2)}) copy-start(bf16[2,1024]{1,0:T(2,128)(2,1)} %chirp_hbm.1) | copy-start | bytes 12292
  0.7 1.9 %copy-start.2 = (s32[4,128]{1,0:T(4,128)S(1)}, s32[4,128]{1,0:T(4,128)}, u32[]{:S(2)}) copy-start(s32[4,128]{1,0:T(4,128)} %index_hbm.1) | copy-start | bytes 6148

commit v5 on v4

--- a/solution.py
+++ b/solution.py
@@ -117,7 +117,7 @@
     pick_ref[...] = (lax.broadcasted_iota(jnp.int32, (64, 64), 1) == code + entry % 2).astype(F32).astype(BF16)
 
     def correlate(window, jj, t):
-        first = (z // 4 + t) % 2
+        first = (z // 4 + t + 1) % 2
         pieces = []
         for c in range(2):
             for kk in range(2):
@@ -137,7 +137,7 @@
                     yb[slot, x, 1] = imag[r0 : r0 + 32]
 
     def send_first(jj, t):
-        first = (z // 4 + t) % 2
+        first = (z // 4 + t + 1) % 2
 
         def send(i, carry):
             k, dest = first + 2 * (i // 4), (y + i) % 4
@@ -163,7 +163,15 @@
 
     @pl.when(is_source)
     def _():
-        correlate(w0, 0, 0)
+        def first_half(t, carry):
+            correlate(w0, 0, t)
+            return carry
+
+        lax.fori_loop(0, 2, first_half, 0)
+        for c in range(2):
+            for r0 in (0, 16):
+                tail = jnp.concatenate([planar_ref[c, r0 : r0 + 16, 4096:], jnp.zeros((16, HALO), BF16)], axis=1)
+                w1[c, r0 : r0 + 16, :] = shifted(tail)
 
     @pl.when(sa == 0)
     def _():
@@ -201,6 +209,9 @@
     eye = (
         lax.broadcasted_iota(jnp.int32, (128, 128), 0) == lax.broadcasted_iota(jnp.int32, (128, 128), 1)
     ).astype(BF16)
+
+    def far_first(t):
+        return (z // 4 + jnp.where(t < 2, 1 + 2 * t, 6 - 2 * t)) % 4
 
     def pass_on(k):
         pltpu.make_async_copy(xr.at[k], xr.at[k], rx.at[k]).wait()
@@ -232,16 +243,19 @@
     @pl.when(is_source)
     def _():
         send_first(0, 0)
-        correlate(w0, 0, 1)
         send_first(0, 1)
-        for c in range(2):
-            for r0 in (0, 16):
-                tail = jnp.concatenate([planar_ref[c, r0 : r0 + 16, 4096:], jnp.zeros((16, HALO), BF16)], axis=1)
-                w1[c, r0 : r0 + 16, :] = shifted(tail)
-        pltpu.make_async_copy(hb, hb, rh).wait()
-        w1[:, :, REACH - HALO :] = w1[:, :, REACH - HALO :] + hb[...]
 
         def second_half(t, carry):
+            @pl.when(sa == 0)
+            def _():
+                pass_on(far_first(2 * t))
+                pass_on(far_first(2 * t + 1))
+
+            @pl.when(t == 0)
+            def _():
+                pltpu.make_async_copy(hb, hb, rh).wait()
+                w1[:, :, REACH - HALO :] = w1[:, :, REACH - HALO :] + hb[...]
+
             correlate(w1, 1, t)
             send_first(1, t)
             return carry
@@ -264,10 +278,10 @@
     pltpu.make_async_copy(rs.at[here], rz.at[here], rzrow).start()
 
     def rest(t, carry):
-        pass_on((z // 4 + t // 2) % 2 + 2 * (t % 2))
-        return carry
-
-    lax.fori_loop(0, 4, rest, 0)
+        pass_on(far_first(t))
+        return carry
+
+    lax.fori_loop(jnp.where(sa == 0, 4, 0), 4, rest, 0)
 
     pltpu.make_async_copy(rz, rz, rzrow).wait()
     row_ref[...] = jnp.sum(rz[...], axis=0)

time: 59.5 us -> 60.2 us (1.012)
  the two profiles are of different devices: /device:TPU:3 before, /device:TPU:35 now
where the time goes in v5:
time: 60.2 us; the launch traced here: 60 us
  Pallas kernels  55.7 us (93%)
  local copies, waits for them, and re-layouts  3.61 us (6%)
  between operations  0.72 us (1%)
    pallas_call x1, Pallas kernels, on_device(): pl.pallas_call(turn_kernel, out_shape=(jax.ShapeDtypeStruct((2, 32, 32, 1...  54.6 us
    unnamed x7, local copies, waits for them, and re-layouts  1.83 us
    broadcast_in_dim x1, local copies, waits for them, and re-layouts, on_device(): return jnp.transpose(image, (1, 0, 2))[None]  1.78 us

profile of v5, /device:TPU:35, one launch (start us, length us, event | category | flops | bytes accessed | tf_op | source)
XLA Modules:
  0.0 60.0 jit_solution(16047999956290632300)
XLA Ops:
  0.7 0.0 copy-start
  0.7 0.0 copy-start.1
  0.7 0.0 copy-start.2
  0.7 1.8 %copy.9 = bf16[32,2,8192]{2,0,1:T(8,128)(2,1)S(1)} copy(bf16[32,2,8192]{2,1,0:T(2,128)(2,1)} %param.5) | data formatting | bytes 2097152 | tf_op args[0]
  2.5 0.0 copy-done
  2.5 0.0 copy-done.1
  2.5 0.0 copy-done.2
  2.5 54.6 %corner_turn.1 = (bf16[2,32,32,128]{3,2,1,0:T(8,128)(2,1)S(1)}, f32[2,512]{1,0:T(2,128)S(1)}) custom-call(s32[1]{0:T(128)S(6)} %copy.10.start_ref, s32[4,128]{1,0:T(4,128)S(1)} %copy-done.2, bf16[2,1024]{1,0:T(2,128)(2,1)S(1)} %copy-done.1, bf16[2,32,8192]{2,1,0:T(8,128)(2,1)S(1)} %bitcast.6, bf16[8,2,512]{2,1,0:T(2,128)(2,1)S(1)} %copy-done), custom_call_target="tpu_custom_call" | custom-call | tf_op jit(solution)/shard_map/corner_turn/pallas_call | solution.py:342
  57.1 1.1 %azimuth_correlate.1 = f32[2,32,4096]{2,1,0:T(8,128)S(1)} custom-call(bf16[2,32,32,128]{3,2,1,0:T(8,128)(2,1)S(1)} %get-tuple-element.7.turned_ref, f32[2,512]{1,0:T(2,128)S(1)} %get-tuple-element.8.row_ref), custom_call_target="tpu_custom_call" | custom-call | tf_op jit(solution)/shard_map/azimuth_correlate/pallas_call | solution.py:371
  58.3 1.8 %copy.7 = f32[1,32,2,4096]{3,2,1,0:T(2,128)} copy(f32[1,32,2,4096]{3,1,2,0:T(8,128)S(1)} %bitcast.7) | data formatting | bytes 2097152 | tf_op jit(solution)/shard_map/broadcast_in_dim | solution.py:380
Async XLA Ops:
  0.7 1.9 %copy-start = (bf16[8,2,512]{2,1,0:T(2,128)(2,1)S(1)}, bf16[8,2,512]{2,1,0:T(2,128)(2,1)}, u32[]{:S(2)}) copy-start(bf16[8,2,512]{2,1,0:T(2,128)(2,1)} %refs_ref.1) | copy-start | bytes 49156
  0.7 1.9 %copy-start.1 = (bf16[2,1024]{1,0:T(2,128)(2,1)S(1)}, bf16[2,1024]{1,0:T(2,128)(2,1)}, u32[]{:S(2)}) copy-start(bf16[2,1024]{1,0:T(2,128)(2,1)} %chirp_hbm.1) | copy-start | bytes 12292
  0.7 1.9 %copy-start.2 = (s32[4,128]{1,0:T(4,128)S(1)}, s32[4,128]{1,0:T(4,128)}, u32[]{:S(2)}) copy-start(s32[4,128]{1,0:T(4,128)} %index_hbm.1) | copy-start | bytes 6148

commit v6 on v5

--- a/solution.py
+++ b/solution.py
@@ -30,6 +30,7 @@
     here = xlo * 16 + z
     across = jnp.where(xhi == 0, xlo, 1 - xlo)
     is_source = xhi == 0
+    place = xlo * 4 + y
 
     get_index = pltpu.make_async_copy(index_hbm, index_ref, sin.at[0])
     get_chirp = pltpu.make_async_copy(chirp_hbm, chirp_ref, sin.at[1])
@@ -38,25 +39,21 @@
 
     barrier = pltpu.get_barrier_semaphore()
 
-    def greet_source(i, carry):
-        dev = (across * 16 + z) * 4 + i
-
-        @pl.when(jnp.logical_or(dev != pa, xhi != sa))
-        def _():
+    @pl.when(sa != 0)
+    def _():
+        def greet_source(i, carry):
+            dev = (across * 16 + z) * 4 + i
             pl.semaphore_signal(barrier, inc=1, device_id=(dev, xhi), device_id_type=MESH)
-
-        return carry
-
-    lax.fori_loop(0, 4, greet_source, 0)
-
-    @pl.when(sa != 0)
-    def _():
-        def greet_y(i, carry):
-            dev = here * 4 + (y + i) % 4
-            pl.semaphore_signal(barrier, inc=1, device_id=(dev, sa), device_id_type=MESH)
-            return carry
-
-        lax.fori_loop(1, 4, greet_y, 0)
+            return carry
+
+        lax.fori_loop(0, 4, greet_source, 0)
+
+    def greet_plane(i, carry):
+        dev = ((i // 3) * 16 + z) * 4 + (y + 1 + i % 3) % 4
+        pl.semaphore_signal(barrier, inc=1, device_id=(dev, sa), device_id_type=MESH)
+        return carry
+
+    lax.fori_loop(0, 6, greet_plane, 0)
 
     def greet_line(i, carry):
         dev = ((here + i) % 32) * 4 + y
@@ -109,12 +106,13 @@
                 halo_ref[c, r0 : r0 + 16, :] = shifted(head)
 
     get_index.wait()
-    entry = lax.broadcasted_iota(jnp.int32, (64, 64), 0)
-    code = jnp.full((64, 64), -2, jnp.int32)
-    for dest in range(32):
-        index = index_ref[sa, 4 * dest + y]
-        code = jnp.where(entry // 2 == dest, jnp.where(index // 32 == pa // 4, 2 * (index % 32), -2), code)
-    pick_ref[...] = (lax.broadcasted_iota(jnp.int32, (64, 64), 1) == code + entry % 2).astype(F32).astype(BF16)
+    entry = lax.broadcasted_iota(jnp.int32, (32, 128), 0)
+    code = jnp.full((32, 128), -2, jnp.int32)
+    for dest in range(16):
+        index = index_ref[sa, xlo * 64 + 4 * dest + y]
+        slot = (index // 512) * 32 + index % 32
+        code = jnp.where(entry // 2 == dest, jnp.where((index // 32) % 16 == z, 2 * slot, -2), code)
+    pick_ref[...] = (lax.broadcasted_iota(jnp.int32, (32, 128), 1) == code + entry % 2).astype(F32).astype(BF16)
 
     def correlate(window, jj, t):
         first = (z // 4 + t + 1) % 2
@@ -175,19 +173,19 @@
 
     @pl.when(sa == 0)
     def _():
+        pl.semaphore_wait(barrier, 41)
+
+    @pl.when(sa == 1)
+    def _():
+        pl.semaphore_wait(barrier, 46)
+
+    @pl.when(sa == 2)
+    def _():
         pl.semaphore_wait(barrier, 38)
 
-    @pl.when(sa == 1)
-    def _():
-        pl.semaphore_wait(barrier, 43)
-
-    @pl.when(sa == 2)
-    def _():
-        pl.semaphore_wait(barrier, 35)
-
     @pl.when(sa == 3)
     def _():
-        pl.semaphore_wait(barrier, 34)
+        pl.semaphore_wait(barrier, 37)
 
     @pl.when(jnp.logical_or(sa == 1, sa == 2))
     def _():
@@ -197,14 +195,15 @@
         ).start()
 
     def row_send(i, carry):
-        dev = here * 4 + (y + i) % 4
+        there = (place + i) % 8
         pltpu.make_async_remote_copy(
-            refs_ref, ga.at[y], srow, rrow, device_id=(dev, sa), device_id_type=MESH
+            refs_ref, ga.at[place], srow, rrow,
+            device_id=(((there // 4) * 16 + z) * 4 + there % 4, sa), device_id_type=MESH,
         ).start()
         return carry
 
-    lax.fori_loop(1, 4, row_send, 0)
-    pltpu.make_async_copy(refs_ref, ga.at[y], rrow).start()
+    lax.fori_loop(1, 8, row_send, 0)
+    pltpu.make_async_copy(refs_ref, ga.at[place], rrow).start()
 
     eye = (
         lax.broadcasted_iota(jnp.int32, (128, 128), 0) == lax.broadcasted_iota(jnp.int32, (128, 128), 1)
@@ -263,19 +262,20 @@
         lax.fori_loop(0, 2, second_half, 0)
 
     pltpu.make_async_copy(ga, ga, rrow).wait()
-    wanted = jnp.dot(pick_ref[...], ga[...].reshape(64, 512), preferred_element_type=F32)
-    for dest in range(32):
-        rs[dest] = wanted[2 * dest : 2 * dest + 2]
+    wanted = jnp.dot(pick_ref[...], ga[...].reshape(128, 512), preferred_element_type=F32)
+    for dest in range(16):
+        rs[dest] = wanted[2 * dest : 2 * dest + 2].astype(BF16)
 
     def row_pass(i, carry):
-        dest = (here + i) % 32
+        dest = (z + i) % 16
         pltpu.make_async_remote_copy(
-            rs.at[dest], rz.at[here], szrow, rzrow, device_id=(dest * 4 + y, sa), device_id_type=MESH
+            rs.at[dest], rz.at[z], szrow, rzrow,
+            device_id=((xlo * 16 + dest) * 4 + y, sa), device_id_type=MESH,
         ).start()
         return carry
 
-    lax.fori_loop(1, 32, row_pass, 0)
-    pltpu.make_async_copy(rs.at[here], rz.at[here], rzrow).start()
+    lax.fori_loop(1, 16, row_pass, 0)
+    pltpu.make_async_copy(rs.at[z], rz.at[z], rzrow).start()
 
     def rest(t, carry):
         pass_on(far_first(t))
@@ -284,12 +284,12 @@
     lax.fori_loop(jnp.where(sa == 0, 4, 0), 4, rest, 0)
 
     pltpu.make_async_copy(rz, rz, rzrow).wait()
-    row_ref[...] = jnp.sum(rz[...], axis=0)
+    row_ref[...] = jnp.sum(rz[...].astype(F32), axis=0)
 
     pltpu.make_async_copy(turned_ref, turned_ref, rzs).wait()
     pltpu.make_async_copy(zs.at[pl.ds(0, 31)], zs.at[pl.ds(0, 31)], sz).wait()
-    pltpu.make_async_copy(rs.at[pl.ds(0, 31)], rs.at[pl.ds(0, 31)], szrow).wait()
-    pltpu.make_async_copy(ga.at[pl.ds(0, 3)], ga.at[pl.ds(0, 3)], srow).wait()
+    pltpu.make_async_copy(rs.at[pl.ds(0, 15)], rs.at[pl.ds(0, 15)], szrow).wait()
+    pltpu.make_async_copy(ga.at[pl.ds(0, 7)], ga.at[pl.ds(0, 7)], srow).wait()
 
     @pl.when(jnp.logical_or(sa == 1, sa == 2))
     def _():
@@ -328,8 +328,8 @@
     real = got[0][:, :256] + got[1][:, 256:]
     imag = got[1][:, :256] - got[0][:, 256:]
     for block in range(16):
-        out_ref[0, :, 256 * block : 256 * block + 256] = real[32 * block : 32 * block + 32]
-        out_ref[1, :, 256 * block : 256 * block + 256] = imag[32 * block : 32 * block + 32]
+        out_ref[:, 0, 256 * block : 256 * block + 256] = real[32 * block : 32 * block + 32]
+        out_ref[:, 1, 256 * block : 256 * block + 256] = imag[32 * block : 32 * block + 32]
 
 
 def params(**more):
@@ -351,7 +351,7 @@
             pltpu.SMEM((4, 128), jnp.int32),
             pltpu.VMEM((2, 1024), BF16),
             pltpu.VMEM((4, 256, SPAN), BF16),
-            pltpu.VMEM((64, 64), BF16),
+            pltpu.VMEM((32, 128), BF16),
             pltpu.VMEM((2, 32, REACH), BF16),
             pltpu.VMEM((2, 32, REACH), BF16),
             pltpu.VMEM((2, 32, HALO), BF16),
@@ -359,9 +359,9 @@
             pltpu.VMEM((32, 2, 2, 32, 128), BF16),
             pltpu.VMEM((4, 2, 2, 4, 32, 128), BF16),
             pltpu.VMEM((32, 2, 32, 128), BF16),
-            pltpu.VMEM((4, 8, 2, 512), BF16),
-            pltpu.VMEM((32, 2, 512), F32),
-            pltpu.VMEM((32, 2, 512), F32),
+            pltpu.VMEM((8, 8, 2, 512), BF16),
+            pltpu.VMEM((16, 2, 512), BF16),
+            pltpu.VMEM((16, 2, 512), BF16),
             dma((2,)), dma, dma, dma, dma((4,)), dma, dma, dma, dma, dma, dma,
         ],
         compiler_params=params(collective_id=0, has_side_effects=True),
@@ -370,14 +370,14 @@
 
     image = pl.pallas_call(
         azimuth_kernel,
-        out_shape=jax.ShapeDtypeStruct((2, 32, 4096), F32),
+        out_shape=jax.ShapeDtypeStruct((32, 2, 4096), F32),
         in_specs=[VMEM, VMEM],
         out_specs=VMEM,
         scratch_shapes=[pltpu.VMEM((2, 18, 32, 256), BF16), pltpu.VMEM((512, 768), BF16)],
         compiler_params=params(),
         name="azimuth_correlate",
     )(turned, row)
-    return jnp.transpose(image, (1, 0, 2))[None]
+    return image[None]
 
 
 def solution(mesh):

time: 60.2 us -> 56.6 us (0.940)
  the two profiles are of different devices: /device:TPU:35 before, /device:TPU:71 now
where the time goes in v6:
time: 56.6 us; the launch traced here: 56.5 us
  Pallas kernels  53.9 us (95%)
  local copies, waits for them, and re-layouts  1.83 us (3%)
  between operations  0.71 us (1%)
    pallas_call x1, Pallas kernels, on_device(): pl.pallas_call(turn_kernel, out_shape=(jax.ShapeDtypeStruct((2, 32, 32, 1...  51.5 us
    pallas_call x1, Pallas kernels, on_device(): pl.pallas_call(azimuth_kernel, out_shape=jax.ShapeDtypeStruct((32, 2, 409...  2.4 us
    unnamed x7, local copies, waits for them, and re-layouts  1.83 us

profile of v6, /device:TPU:71, one launch (start us, length us, event | category | flops | bytes accessed | tf_op | source)
XLA Modules:
  0.0 56.5 jit_solution(5096928968431038086)
XLA Ops:
  0.7 0.0 copy-start
  0.7 0.0 copy-start.1
  0.7 0.0 copy-start.2
  0.7 1.8 %copy.8 = bf16[32,2,8192]{2,0,1:T(8,128)(2,1)S(1)} copy(bf16[32,2,8192]{2,1,0:T(2,128)(2,1)} %param.5) | data formatting | bytes 2097152 | tf_op args[0]
  2.5 0.0 copy-done
  2.5 0.0 copy-done.1
  2.5 0.0 copy-done.2
  2.5 51.5 %corner_turn.1 = (bf16[2,32,32,128]{3,2,1,0:T(8,128)(2,1)S(1)}, f32[2,512]{1,0:T(2,128)S(1)}) custom-call(s32[1]{0:T(128)S(6)} %copy.9.start_ref, s32[4,128]{1,0:T(4,128)S(1)} %copy-done.2, bf16[2,1024]{1,0:T(2,128)(2,1)S(1)} %copy-done.1, bf16[2,32,8192]{2,1,0:T(8,128)(2,1)S(1)} %bitcast.4, bf16[8,2,512]{2,1,0:T(2,128)(2,1)S(1)} %copy-done), custom_call_target="tpu_custom_call" | custom-call | tf_op jit(solution)/shard_map/corner_turn/pallas_call | solution.py:342
  54.1 2.4 %azimuth_correlate.1 = f32[32,2,4096]{2,1,0:T(2,128)} custom-call(bf16[2,32,32,128]{3,2,1,0:T(8,128)(2,1)S(1)} %get-tuple-element.7.turned_ref, f32[2,512]{1,0:T(2,128)S(1)} %get-tuple-element.8.row_ref), custom_call_target="tpu_custom_call" | custom-call | tf_op jit(solution)/shard_map/azimuth_correlate/pallas_call | solution.py:371
Async XLA Ops:
  0.7 1.9 %copy-start = (bf16[8,2,512]{2,1,0:T(2,128)(2,1)S(1)}, bf16[8,2,512]{2,1,0:T(2,128)(2,1)}, u32[]{:S(2)}) copy-start(bf16[8,2,512]{2,1,0:T(2,128)(2,1)} %refs_ref.1) | copy-start | bytes 49156
  0.7 1.9 %copy-start.1 = (bf16[2,1024]{1,0:T(2,128)(2,1)S(1)}, bf16[2,1024]{1,0:T(2,128)(2,1)}, u32[]{:S(2)}) copy-start(bf16[2,1024]{1,0:T(2,128)(2,1)} %chirp_hbm.1) | copy-start | bytes 12292
  0.7 1.9 %copy-start.2 = (s32[4,128]{1,0:T(4,128)S(1)}, s32[4,128]{1,0:T(4,128)}, u32[]{:S(2)}) copy-start(s32[4,128]{1,0:T(4,128)} %index_hbm.1) | copy-start | bytes 6148

commit v7 on v6

--- a/solution.py
+++ b/solution.py
@@ -17,11 +17,12 @@
 VMEM = pl.BlockSpec(memory_space=pltpu.VMEM)
 SMEM = pl.BlockSpec(memory_space=pltpu.SMEM)
 ANY = pl.BlockSpec(memory_space=pl.ANY)
+HBM = pl.BlockSpec(memory_space=pltpu.HBM)
 
 
 def turn_kernel(
-    start_ref, index_hbm, chirp_hbm, planar_ref, refs_ref, turned_ref, row_ref,
-    index_ref, chirp_ref, taps_ref, pick_ref, w0, w1, halo_ref, hb, yb, xr, zs, ga, rs, rz, sin, sh, rh, sx, rx, sz, rzs, srow, rrow, szrow, rzrow,
+    start_ref, index_hbm, chirp_hbm, raw_hbm, refs_ref, turned_ref, row_ref,
+    raw_ref, planar_ref, index_ref, chirp_ref, taps_ref, pick_ref, w0, w1, halo_ref, hb, yb, xr, zs, ga, rs, rz, sraw, sin, sh, rh, sx, rx, sz, rzs, srow, rrow, szrow, rzrow,
 ):
     pa = lax.axis_index("pa")
     sa = lax.axis_index("sa")
@@ -34,8 +35,15 @@
 
     get_index = pltpu.make_async_copy(index_hbm, index_ref, sin.at[0])
     get_chirp = pltpu.make_async_copy(chirp_hbm, chirp_ref, sin.at[1])
+    get_chirp.start()
     get_index.start()
-    get_chirp.start()
+
+    def get_raw(q):
+        part = pl.ds(2048 * q, 2048)
+        return pltpu.make_async_copy(raw_hbm.at[:, :, part], raw_ref.at[:, :, part], sraw.at[q])
+
+    for q in range(4):
+        get_raw(q).start()
 
     barrier = pltpu.get_barrier_semaphore()
 
@@ -94,16 +102,6 @@
                     taps_ref[dest, r0 : r0 + 32, 128 * g : 128 * g + 1280] = wide[32 * dest : 32 * dest + 32, :]
                     if g < 3:
                         taps_ref[dest, r0 : r0 + 32, 128 * g + 1280 :] = jnp.zeros((32, 384 - 128 * g), BF16)
-        for c in range(2):
-            for r0 in (0, 16):
-                w0[c, r0 : r0 + 16, :] = shifted(planar_ref[c, r0 : r0 + 16, :7168])
-
-    @pl.when(jnp.logical_or(sa == 1, sa == 2))
-    def _():
-        for c in range(2):
-            for r0 in (0, 16):
-                head = jnp.concatenate([jnp.zeros((16, 1920), BF16), planar_ref[c, r0 : r0 + 16, :HALO]], axis=1)
-                halo_ref[c, r0 : r0 + 16, :] = shifted(head)
 
     get_index.wait()
     entry = lax.broadcasted_iota(jnp.int32, (32, 128), 0)
@@ -113,6 +111,23 @@
         slot = (index // 512) * 32 + index % 32
         code = jnp.where(entry // 2 == dest, jnp.where((index // 32) % 16 == z, 2 * slot, -2), code)
     pick_ref[...] = (lax.broadcasted_iota(jnp.int32, (32, 128), 1) == code + entry % 2).astype(F32).astype(BF16)
+
+    source_row = lax.broadcasted_iota(jnp.int32, (64, 64), 1)
+    target_row = lax.broadcasted_iota(jnp.int32, (64, 64), 0)
+    apart = (source_row == 2 * (target_row % 32) + target_row // 32).astype(F32).astype(BF16)
+    for q in range(4):
+        get_raw(q).wait()
+        rows = raw_ref[:, :, 2048 * q : 2048 * q + 2048].reshape(64, 2048)
+        rows = jnp.dot(apart, rows, preferred_element_type=F32).astype(BF16)
+        planar_ref[0, :, 2048 * q : 2048 * q + 2048] = rows[:32]
+        planar_ref[1, :, 2048 * q : 2048 * q + 2048] = rows[32:]
+
+    @pl.when(jnp.logical_or(sa == 1, sa == 2))
+    def _():
+        for c in range(2):
+            for r0 in (0, 16):
+                head = jnp.concatenate([jnp.zeros((16, 1920), BF16), planar_ref[c, r0 : r0 + 16, :HALO]], axis=1)
+                halo_ref[c, r0 : r0 + 16, :] = shifted(head)
 
     def correlate(window, jj, t):
         first = (z // 4 + t + 1) % 2
@@ -161,6 +176,10 @@
 
     @pl.when(is_source)
     def _():
+        for c in range(2):
+            for r0 in (0, 16):
+                w0[c, r0 : r0 + 16, :] = shifted(planar_ref[c, r0 : r0 + 16, :7168])
+
         def first_half(t, carry):
             correlate(w0, 0, t)
             return carry
@@ -304,32 +323,39 @@
         pltpu.make_async_copy(yb, yb, sx).wait()
 
 
-def azimuth_kernel(turned_ref, row_ref, out_ref, lhs, taps):
+def azimuth_kernel(turned_ref, row_ref, out_ref, lhs, taps, image, sems):
     zeros = jnp.zeros((32, 256), BF16)
     for c in range(2):
         lhs[c, 0] = zeros
         lhs[c, 17] = zeros
         for block in range(16):
             for half in range(2):
-                tile = turned_ref[c, 2 * block + half]
-                lhs[c, block + 1, :, 128 * half : 128 * half + 128] = tile
+                lhs[c, block + 1, :, 128 * half : 128 * half + 128] = turned_ref[c, 2 * block + half]
     for part in range(2):
         row = jnp.concatenate([row_ref[part : part + 1, :], jnp.zeros((1, 512), F32)], axis=1)
         wide = pltpu.roll(jnp.broadcast_to(row, (256, 1024)), 0, 1, stride=1, stride_axis=0)
         taps[256 * part : 256 * part + 256, :] = wide[:, :768].astype(BF16)
-    got = []
-    for c in range(2):
-        total = None
-        for o in range(3):
-            rows = lhs[c, o : o + 16].reshape(512, 256)
-            piece = lax.dot_general(rows, taps[:, 256 * o : 256 * o + 256], NT, preferred_element_type=F32)
-            total = piece if total is None else total + piece
-        got.append(total)
-    real = got[0][:, :256] + got[1][:, 256:]
-    imag = got[1][:, :256] - got[0][:, 256:]
-    for block in range(16):
-        out_ref[:, 0, 256 * block : 256 * block + 256] = real[32 * block : 32 * block + 32]
-        out_ref[:, 1, 256 * block : 256 * block + 256] = imag[32 * block : 32 * block + 32]
+    copies = []
+    for side in range(2):
+        got = []
+        for c in range(2):
+            total = None
+            for o in range(3):
+                rows = lhs[c, 8 * side + o : 8 * side + o + 8].reshape(256, 256)
+                piece = lax.dot_general(rows, taps[:, 256 * o : 256 * o + 256], NT, preferred_element_type=F32)
+                total = piece if total is None else total + piece
+            got.append(total)
+        real = got[0][:, :256] + got[1][:, 256:]
+        imag = got[1][:, :256] - got[0][:, 256:]
+        for block in range(8):
+            image[side, :, 0, 256 * block : 256 * block + 256] = real[32 * block : 32 * block + 32]
+            image[side, :, 1, 256 * block : 256 * block + 256] = imag[32 * block : 32 * block + 32]
+        copies.append(
+            pltpu.make_async_copy(image.at[side], out_ref.at[:, :, pl.ds(2048 * side, 2048)], sems.at[side])
+        )
+        copies[-1].start()
+    for copy in copies:
+        copy.wait()
 
 
 def params(**more):
@@ -337,7 +363,8 @@
 
 
 def on_device(raw_echo, chirp_replica, azimuth_refs, migration_index, window_start):
-    planar = jnp.transpose(raw_echo, (1, 0, 2))
+    large = (migration_index, chirp_replica, raw_echo, azimuth_refs)
+    in_hbm = [pltpu.with_memory_space_constraint(value, pltpu.HBM) for value in large]
     dma = pltpu.SemaphoreType.DMA
     turned, row = pl.pallas_call(
         turn_kernel,
@@ -345,9 +372,11 @@
             jax.ShapeDtypeStruct((2, 32, 32, 128), BF16),
             jax.ShapeDtypeStruct((2, 512), F32),
         ),
-        in_specs=[SMEM, ANY, ANY, VMEM, ANY],
+        in_specs=[SMEM, HBM, HBM, HBM, HBM],
         out_specs=(ANY, VMEM),
         scratch_shapes=[
+            pltpu.VMEM((32, 2, 8192), BF16),
+            pltpu.VMEM((2, 32, 8192), BF16),
             pltpu.SMEM((4, 128), jnp.int32),
             pltpu.VMEM((2, 1024), BF16),
             pltpu.VMEM((4, 256, SPAN), BF16),
@@ -362,18 +391,23 @@
             pltpu.VMEM((8, 8, 2, 512), BF16),
             pltpu.VMEM((16, 2, 512), BF16),
             pltpu.VMEM((16, 2, 512), BF16),
-            dma((2,)), dma, dma, dma, dma((4,)), dma, dma, dma, dma, dma, dma,
+            dma((4,)), dma((2,)), dma, dma, dma, dma((4,)), dma, dma, dma, dma, dma, dma,
         ],
         compiler_params=params(collective_id=0, has_side_effects=True),
         name="corner_turn",
-    )(window_start, migration_index, chirp_replica, planar, azimuth_refs)
+    )(window_start, *in_hbm)
 
     image = pl.pallas_call(
         azimuth_kernel,
         out_shape=jax.ShapeDtypeStruct((32, 2, 4096), F32),
         in_specs=[VMEM, VMEM],
-        out_specs=VMEM,
-        scratch_shapes=[pltpu.VMEM((2, 18, 32, 256), BF16), pltpu.VMEM((512, 768), BF16)],
+        out_specs=HBM,
+        scratch_shapes=[
+            pltpu.VMEM((2, 18, 32, 256), BF16),
+            pltpu.VMEM((512, 768), BF16),
+            pltpu.VMEM((2, 32, 2, 2048), F32),
+            dma((2,)),
+        ],
         compiler_params=params(),
         name="azimuth_correlate",
     )(turned, row)

time: 56.6 us -> 55.5 us (0.981)
  the two profiles are of different devices: /device:TPU:71 before, /device:TPU:39 now
where the time goes in v7:
time: 55.5 us; the launch traced here: 55.3 us
  Pallas kernels  54.7 us (99%)
  between operations  0.66 us (1%)
    pallas_call x1, Pallas kernels, on_device(): pl.pallas_call(turn_kernel, out_shape=(jax.ShapeDtypeStruct((2, 32, 32, 1...  52.4 us
    pallas_call x1, Pallas kernels, on_device(): pl.pallas_call(azimuth_kernel, out_shape=jax.ShapeDtypeStruct((32, 2, 409...  2.24 us

profile of v7, /device:TPU:39, one launch (start us, length us, event | category | flops | bytes accessed | tf_op | source)
XLA Modules:
  0.0 55.3 jit_solution(2948288802674978145)
XLA Ops:
  0.7 52.4 %corner_turn.1 = (bf16[2,32,32,128]{3,2,1,0:T(8,128)(2,1)S(1)}, f32[2,512]{1,0:T(2,128)S(1)}) custom-call(s32[1]{0:T(128)S(6)} %copy.6.start_ref, s32[4,128]{1,0:T(4,128)} %index_hbm.1, bf16[2,1024]{1,0:T(2,128)(2,1)} %chirp_hbm.1, bf16[32,2,8192]{2,1,0:T(2,128)(2,1)} %raw_hbm.1, bf16[8,2,512]{2,1,0:T(2,128)(2,1)} %refs_ref.1), custom_call_target="tpu_custom_call" | custom-call | tf_op jit(solution)/shard_map/corner_turn/pallas_call | solution.py:369
  53.1 2.2 %azimuth_correlate.1 = f32[32,2,4096]{2,1,0:T(2,128)} custom-call(bf16[2,32,32,128]{3,2,1,0:T(8,128)(2,1)S(1)} %get-tuple-element.7.turned_ref, f32[2,512]{1,0:T(2,128)S(1)} %get-tuple-element.8.row_ref), custom_call_target="tpu_custom_call" | custom-call | tf_op jit(solution)/shard_map/azimuth_correlate/pallas_call | solution.py:400

commit v8 on v7

--- a/solution.py
+++ b/solution.py
@@ -162,13 +162,13 @@
             @pl.when(there)
             def _():
                 pltpu.make_async_remote_copy(
-                    yb.at[slot], xr.at[k, :, :, y], sx, rx.at[k],
+                    yb.at[slot], xr.at[k, y], sx, rx.at[k],
                     device_id=(dev, target), device_id_type=MESH,
                 ).start()
 
             @pl.when(jnp.logical_not(there))
             def _():
-                pltpu.make_async_copy(yb.at[slot], xr.at[k, :, :, y], rx.at[k]).start()
+                pltpu.make_async_copy(yb.at[slot], xr.at[k, y], rx.at[k]).start()
 
             return carry
 
@@ -234,7 +234,7 @@
     def pass_on(k):
         pltpu.make_async_copy(xr.at[k], xr.at[k], rx.at[k]).wait()
         for x in range(2):
-            pulses = xr[k, x].reshape(256, 128)
+            pulses = jnp.concatenate([xr[k, :, x, c].reshape(128, 128) for c in range(2)], axis=0)
             flipped = lax.dot_general(eye, pulses, NT, preferred_element_type=F32).astype(BF16)
             for g in range(4):
                 for c in range(2):
@@ -246,13 +246,13 @@
             @pl.when(dest != here)
             def _():
                 pltpu.make_async_remote_copy(
-                    zs.at[dest], turned_ref.at[:, across * 16 + z], sz, rzs,
+                    zs.at[dest], turned_ref.at[across * 16 + z], sz, rzs,
                     device_id=(dest * 4 + y, sa), device_id_type=MESH,
                 ).start()
 
             @pl.when(dest == here)
             def _():
-                pltpu.make_async_copy(zs.at[dest], turned_ref.at[:, across * 16 + z], rzs).start()
+                pltpu.make_async_copy(zs.at[dest], turned_ref.at[across * 16 + z], rzs).start()
 
             return carry
 
@@ -279,6 +279,12 @@
             return carry
 
         lax.fori_loop(0, 2, second_half, 0)
+
+    def rest(t, carry):
+        pass_on(far_first(t))
+        return carry
+
+    lax.fori_loop(jnp.where(sa == 0, 2, 0), 2, rest, 0)
 
     pltpu.make_async_copy(ga, ga, rrow).wait()
     wanted = jnp.dot(pick_ref[...], ga[...].reshape(128, 512), preferred_element_type=F32)
@@ -296,11 +302,7 @@
     lax.fori_loop(1, 16, row_pass, 0)
     pltpu.make_async_copy(rs.at[z], rz.at[z], rzrow).start()
 
-    def rest(t, carry):
-        pass_on(far_first(t))
-        return carry
-
-    lax.fori_loop(jnp.where(sa == 0, 4, 0), 4, rest, 0)
+    lax.fori_loop(jnp.where(sa == 0, 4, 2), 4, rest, 0)
 
     pltpu.make_async_copy(rz, rz, rzrow).wait()
     row_ref[...] = jnp.sum(rz[...].astype(F32), axis=0)
@@ -330,7 +332,7 @@
         lhs[c, 17] = zeros
         for block in range(16):
             for half in range(2):
-                lhs[c, block + 1, :, 128 * half : 128 * half + 128] = turned_ref[c, 2 * block + half]
+                lhs[c, block + 1, :, 128 * half : 128 * half + 128] = turned_ref[2 * block + half, c]
     for part in range(2):
         row = jnp.concatenate([row_ref[part : part + 1, :], jnp.zeros((1, 512), F32)], axis=1)
         wide = pltpu.roll(jnp.broadcast_to(row, (256, 1024)), 0, 1, stride=1, stride_axis=0)
@@ -369,7 +371,7 @@
     turned, row = pl.pallas_call(
         turn_kernel,
         out_shape=(
-            jax.ShapeDtypeStruct((2, 32, 32, 128), BF16),
+            jax.ShapeDtypeStruct((32, 2, 32, 128), BF16),
             jax.ShapeDtypeStruct((2, 512), F32),
         ),
         in_specs=[SMEM, HBM, HBM, HBM, HBM],
@@ -386,7 +388,7 @@
             pltpu.VMEM((2, 32, HALO), BF16),
             pltpu.VMEM((2, 32, HALO), BF16),
             pltpu.VMEM((32, 2, 2, 32, 128), BF16),
-            pltpu.VMEM((4, 2, 2, 4, 32, 128), BF16),
+            pltpu.VMEM((4, 4, 2, 2, 32, 128), BF16),
             pltpu.VMEM((32, 2, 32, 128), BF16),
             pltpu.VMEM((8, 8, 2, 512), BF16),
             pltpu.VMEM((16, 2, 512), BF16),

time: 55.5 us -> 54.6 us (0.984)
  the two profiles are of different devices: /device:TPU:39 before, /device:TPU:35 now
where the time goes in v8:
time: 54.6 us; the launch traced here: 54.5 us
  Pallas kernels  53.8 us (99%)
  between operations  0.66 us (1%)
    pallas_call x1, Pallas kernels, on_device(): pl.pallas_call(turn_kernel, out_shape=(jax.ShapeDtypeStruct((32, 2, 32, 1...  51.6 us
    pallas_call x1, Pallas kernels, on_device(): pl.pallas_call(azimuth_kernel, out_shape=jax.ShapeDtypeStruct((32, 2, 409...  2.24 us

profile of v8, /device:TPU:35, one launch (start us, length us, event | category | flops | bytes accessed | tf_op | source)
XLA Modules:
  0.0 54.5 jit_solution(13835125786868060552)
XLA Ops:
  0.7 51.6 %corner_turn.1 = (bf16[32,2,32,128]{3,2,1,0:T(8,128)(2,1)S(1)}, f32[2,512]{1,0:T(2,128)S(1)}) custom-call(s32[1]{0:T(128)S(6)} %copy.6.start_ref, s32[4,128]{1,0:T(4,128)} %index_hbm.1, bf16[2,1024]{1,0:T(2,128)(2,1)} %chirp_hbm.1, bf16[32,2,8192]{2,1,0:T(2,128)(2,1)} %raw_hbm.1, bf16[8,2,512]{2,1,0:T(2,128)(2,1)} %refs_ref.1), custom_call_target="tpu_custom_call" | custom-call | tf_op jit(solution)/shard_map/corner_turn/pallas_call | solution.py:371
  52.2 2.2 %azimuth_correlate.1 = f32[32,2,4096]{2,1,0:T(2,128)} custom-call(bf16[32,2,32,128]{3,2,1,0:T(8,128)(2,1)S(1)} %get-tuple-element.7.turned_ref, f32[2,512]{1,0:T(2,128)S(1)} %get-tuple-element.8.row_ref), custom_call_target="tpu_custom_call" | custom-call | tf_op jit(solution)/shard_map/azimuth_correlate/pallas_call | solution.py:402

commit v9 on v8

--- a/solution.py
+++ b/solution.py
@@ -208,10 +208,13 @@
 
     @pl.when(jnp.logical_or(sa == 1, sa == 2))
     def _():
-        pltpu.make_async_remote_copy(
-            halo_ref, hb, sh, rh,
-            device_id=(pa, sa - 1), device_id_type=MESH,
-        ).start()
+        for c in range(2):
+            for r0 in (0, 16):
+                piece = (c, pl.ds(r0, 16))
+                pltpu.make_async_remote_copy(
+                    halo_ref.at[piece], hb.at[piece], sh, rh,
+                    device_id=(pa, sa - 1), device_id_type=MESH,
+                ).start()
 
     def row_send(i, carry):
         there = (place + i) % 8

time: 54.6 us -> 54.6 us (level)
  no operation moved by 1% of the time
where the time goes in v9:
time: 54.6 us; the launch traced here: 54.5 us
  Pallas kernels  53.8 us (99%)
  between operations  0.66 us (1%)
    pallas_call x1, Pallas kernels, on_device(): pl.pallas_call(turn_kernel, out_shape=(jax.ShapeDtypeStruct((32, 2, 32, 1...  51.6 us
    pallas_call x1, Pallas kernels, on_device(): pl.pallas_call(azimuth_kernel, out_shape=jax.ShapeDtypeStruct((32, 2, 409...  2.24 us

profile of v9, /device:TPU:35, one launch (start us, length us, event | category | flops | bytes accessed | tf_op | source)
XLA Modules:
  0.0 54.5 jit_solution(6088852226761314152)
XLA Ops:
  0.7 51.6 %corner_turn.1 = (bf16[32,2,32,128]{3,2,1,0:T(8,128)(2,1)S(1)}, f32[2,512]{1,0:T(2,128)S(1)}) custom-call(s32[1]{0:T(128)S(6)} %copy.6.start_ref, s32[4,128]{1,0:T(4,128)} %index_hbm.1, bf16[2,1024]{1,0:T(2,128)(2,1)} %chirp_hbm.1, bf16[32,2,8192]{2,1,0:T(2,128)(2,1)} %raw_hbm.1, bf16[8,2,512]{2,1,0:T(2,128)(2,1)} %refs_ref.1), custom_call_target="tpu_custom_call" | custom-call | tf_op jit(solution)/shard_map/corner_turn/pallas_call | solution.py:374
  52.3 2.2 %azimuth_correlate.1 = f32[32,2,4096]{2,1,0:T(2,128)} custom-call(bf16[32,2,32,128]{3,2,1,0:T(8,128)(2,1)S(1)} %get-tuple-element.7.turned_ref, f32[2,512]{1,0:T(2,128)S(1)} %get-tuple-element.8.row_ref), custom_call_target="tpu_custom_call" | custom-call | tf_op jit(solution)/shard_map/azimuth_correlate/pallas_call | solution.py:405

commit v10 on v8

--- a/solution.py
+++ b/solution.py
@@ -33,6 +33,15 @@
     is_source = xhi == 0
     place = xlo * 4 + y
 
+    barrier = pltpu.get_barrier_semaphore()
+
+    def greet_line(i, carry):
+        dev = ((here + 1 + (i + 7) % 31) % 32) * 4 + y
+        pl.semaphore_signal(barrier, inc=1, device_id=(dev, sa), device_id_type=MESH)
+        return carry
+
+    lax.fori_loop(0, 31, greet_line, 0)
+
     get_index = pltpu.make_async_copy(index_hbm, index_ref, sin.at[0])
     get_chirp = pltpu.make_async_copy(chirp_hbm, chirp_ref, sin.at[1])
     get_chirp.start()
@@ -45,7 +54,6 @@
     for q in range(4):
         get_raw(q).start()
 
-    barrier = pltpu.get_barrier_semaphore()
 
     @pl.when(sa != 0)
     def _():
@@ -62,13 +70,6 @@
         return carry
 
     lax.fori_loop(0, 6, greet_plane, 0)
-
-    def greet_line(i, carry):
-        dev = ((here + i) % 32) * 4 + y
-        pl.semaphore_signal(barrier, inc=1, device_id=(dev, sa), device_id_type=MESH)
-        return carry
-
-    lax.fori_loop(1, 32, greet_line, 0)
 
     @pl.when(sa < 2)
     def _():

time: 54.6 us -> 55.5 us (1.016)
  Pallas kernels: 53.8 us -> 54.7 us
    pallas_call x1, Pallas kernels: 51.6 us -> 52.5 us  [on_device(): pl.pallas_call(turn_kernel, out_shape=(jax.ShapeDtypeStruct((32, 2, 32, 1...]
where the time goes in v10:
time: 55.5 us; the launch traced here: 55.4 us
  Pallas kernels  54.7 us (99%)
  between operations  0.66 us (1%)
    pallas_call x1, Pallas kernels, on_device(): pl.pallas_call(turn_kernel, out_shape=(jax.ShapeDtypeStruct((32, 2, 32, 1...  52.5 us
    pallas_call x1, Pallas kernels, on_device(): pl.pallas_call(azimuth_kernel, out_shape=jax.ShapeDtypeStruct((32, 2, 409...  2.24 us

profile of v10, /device:TPU:35, one launch (start us, length us, event | category | flops | bytes accessed | tf_op | source)
XLA Modules:
  0.0 55.4 jit_solution(4884203843820861762)
XLA Ops:
  0.7 52.5 %corner_turn.1 = (bf16[32,2,32,128]{3,2,1,0:T(8,128)(2,1)S(1)}, f32[2,512]{1,0:T(2,128)S(1)}) custom-call(s32[1]{0:T(128)S(6)} %copy.6.start_ref, s32[4,128]{1,0:T(4,128)} %index_hbm.1, bf16[2,1024]{1,0:T(2,128)(2,1)} %chirp_hbm.1, bf16[32,2,8192]{2,1,0:T(2,128)(2,1)} %raw_hbm.1, bf16[8,2,512]{2,1,0:T(2,128)(2,1)} %refs_ref.1), custom_call_target="tpu_custom_call" | custom-call | tf_op jit(solution)/shard_map/corner_turn/pallas_call | solution.py:372
  53.2 2.2 %azimuth_correlate.1 = f32[32,2,4096]{2,1,0:T(2,128)} custom-call(bf16[32,2,32,128]{3,2,1,0:T(8,128)(2,1)S(1)} %get-tuple-element.7.turned_ref, f32[2,512]{1,0:T(2,128)S(1)} %get-tuple-element.8.row_ref), custom_call_target="tpu_custom_call" | custom-call | tf_op jit(solution)/shard_map/azimuth_correlate/pallas_call | solution.py:403
